TPU v7x, 128 devices: a whole 4x4x4 slice. The times are simulated.
128 devices in a mesh: gx: 8 (over z_hi, y), gy: 4 (over x), gz: 4 (over z_lo, core).
Axes of the slice: x: 4, y: 4, z: 4 (z_hi: 2, z_lo: 2; z = z_hi * 2 + z_lo), core: 2. Of those that a mesh axis runs over, the one named last changes fastest.
Arguments:
- bold_data: bfloat16 [64, 64, 128, 512], P('gx', 'gy', 'gz'), may hold values from -6 to 6
- spatial_maps: float32 [64, 64, 64, 128], P(None, 'gx', 'gy', 'gz'), may hold values from -6 to 6
- live_blocks: int32 [8, 4, 4], P('gx', 'gy', 'gz'), may hold values from 16 to 128, as said below
Outputs:
- new_maps: float32 [64, 64, 64, 128], P(None, 'gx', 'gy', 'gz')
- time_courses: bfloat16 [64, 512], replicated
Inputs may be any that keep to these rules, and one draw needn't show every extreme that they name: live_blocks counts live rows of a device's block; rows are numbered (x mod 8) * 16 + (y mod 16) and the live ones come first.
All inputs are finite; a program needn't handle non-finite values.
Results may differ from a plain program's by a relative error of at most 0.011.
Values may be sent and summed in bfloat16 or wider, within the bound.
A program may use at most 192 MiB of HBM per device.

v0:
```python
import math

import jax
import jax.numpy as jnp
from jax import lax
from jax.sharding import PartitionSpec as P

RADIUS = 8
ITERS = 2


def extended(x, sides, width):
    for axis, dim in sides:
        peers, length = (lax.axis_size(axis), x.shape[dim])
        up = [(i, (i + 1) % peers) for i in range(peers - 1)]
        down = [(j, i) for i, j in up]
        last = lax.slice_in_dim(x, length - width, length, axis=dim)
        leading = lax.slice_in_dim(x, 0, width, axis=dim)
        before = lax.ppermute(last, axis, up)
        after = lax.ppermute(leading, axis, down)
        x = jnp.concatenate([before, x, after], axis=dim)
    return x


def band_matrix(length, dtype):
    total = sum((math.exp(-float(d * d) / 32.0) for d in range(-RADIUS, RADIUS + 1)))
    count = length - 2 * RADIUS
    rows = lax.broadcasted_iota(jnp.int32, (length, count), 0)
    cols = lax.broadcasted_iota(jnp.int32, (length, count), 1)
    offset = (rows - cols - RADIUS).astype(dtype)
    inside = jnp.logical_and(rows - cols >= 0, rows - cols <= 2 * RADIUS)
    return jnp.where(inside, jnp.exp(-offset * offset / 32.0) / total, jnp.zeros_like(offset))


def filter_along(field, axis):
    band = band_matrix(field.shape[axis], field.dtype)
    result = jnp.tensordot(field, band, axes=((axis,), (0,)), precision=lax.Precision.HIGHEST)
    return jnp.moveaxis(result, -1, axis)


def smooth_maps(plain):
    padded = extended(plain, (("gx", 1), ("gy", 2), ("gz", 3)), RADIUS).astype(jnp.float32)
    return filter_along(filter_along(filter_along(padded, 1), 2), 3)


def smooth_grad(plain):
    padded = extended(plain, (("gx", 1), ("gy", 2), ("gz", 3)), RADIUS).astype(jnp.float32)
    return filter_along(filter_along(filter_along(padded, 1), 2), 3)


def per_device(bold_data, spatial_maps, live_blocks):
    chans, size_x, size_y, size_z = spatial_maps.shape
    frame_count = bold_data.shape[3]
    count = live_blocks[0, 0, 0]
    row_ids = lax.broadcasted_iota(jnp.int32, (size_x, size_y), 0) * size_y + lax.broadcasted_iota(
        jnp.int32, (size_x, size_y), 1
    )
    live = jnp.broadcast_to((row_ids < count)[:, :, None], (size_x, size_y, size_z))
    live_half = live.astype(jnp.bfloat16)[None]
    live_flat = live.reshape(1, -1).astype(jnp.float32)
    flat_frames = bold_data.reshape(size_x * size_y * size_z, frame_count)
    all_cells = float(chans * size_x * size_y * size_z * lax.axis_size(("gx", "gy", "gz")))
    weights = spatial_maps.reshape(chans, -1)
    rounded = None
    for step in range(ITERS):
        plain = weights.reshape(chans, size_x, size_y, size_z).astype(jnp.bfloat16)
        filtered = smooth_maps(plain)
        smoothed = filtered.astype(jnp.bfloat16) * live_half
        partial_courses = jnp.dot(
            smoothed.reshape(chans, -1), flat_frames, preferred_element_type=jnp.float32
        )
        courses = lax.psum(partial_courses, ("gx", "gy", "gz"))
        gram = jnp.dot(courses, courses.T, precision=lax.Precision.HIGHEST)
        rounded = courses.astype(jnp.bfloat16)
        trace_value = jnp.trace(gram)
        raw_grad = (
            jnp.dot(rounded, flat_frames.T, preferred_element_type=jnp.float32) * live_flat
        ).astype(jnp.bfloat16)
        grad = smooth_grad(raw_grad.reshape(chans, size_x, size_y, size_z)).reshape(chans, -1)
        energy = lax.psum(jnp.sum(grad * grad), ("gx", "gy", "gz")) / all_cells
        scale = 1.0 / jnp.sqrt(energy + 1e-06)
        decay = jnp.dot(gram, weights, precision=lax.Precision.HIGHEST)
        weights = weights + 0.5 * (grad * scale - float(chans) / trace_value * decay)
    return (weights.reshape(chans, size_x, size_y, size_z), rounded)


def solution(mesh):
    return jax.shard_map(
        per_device,
        mesh=mesh,
        in_specs=(P("gx", "gy", "gz", None), P(None, "gx", "gy", "gz"), P("gx", "gy", "gz")),
        out_specs=(P(None, "gx", "gy", "gz"), P()),
        check_vma=False,
    )
```

profile of v0, /device:TPU:1, one launch (start us, length us, event | category | flops | bytes accessed | tf_op | source)
XLA Modules:
  0.0 1300.3 jit_solution(917846348926183475)
XLA Ops:
  15.1 20.5 %collective-permute-done.1 = bf16[64,8,16,32]{0,3,2,1:T(8,128)(2,1)S(1)} collective-permute-done((bf16[64,8,16,32]{0,3,2,1:T(8,128)(2,1)S(1)}, bf16[64,8,16,32]{0,3,2,1:T(8,128)(2,1)S(1)}, u32[]{:S(2)}, u32[]{:S(2)}) %collective-permute-start.1) | collective-permute-done | bytes 524320 | tf_op jit(solution)/shard_map/ppermute | solution.py:20
  42.6 30.5 %collective-permute-done.2 = bf16[64,24,8,32]{0,3,2,1:T(8,128)(2,1)S(1)} collective-permute-done((bf16[64,24,8,32]{0,3,2,1:T(8,128)(2,1)S(1)}, bf16[64,24,8,32]{0,3,2,1:T(8,128)(2,1)S(1)}, u32[]{:S(2)}, u32[]{:S(2)}) %collective-permute-start.2) | collective-permute-done | bytes 786464 | tf_op jit(solution)/shard_map/ppermute | solution.py:19
  81.7 6.4 collective-permute-start.4
  90.8 14.7 %collective-permute-done.4 = bf16[64,24,32,8]{0,3,2,1:T(8,128)(2,1)S(1)} collective-permute-done((bf16[64,24,32,8]{0,3,2,1:T(8,128)(2,1)S(1)}, bf16[64,24,32,8]{0,3,2,1:T(8,128)(2,1)S(1)}, u32[]{:S(2)}, u32[]{:S(2)}) %collective-permute-start.4) | collective-permute-done | bytes 786464 | tf_op jit(solution)/shard_map/ppermute | solution.py:19
  109.9 13.0 pad_maximum_fusion.3
  122.8 17.0 %copy.102 = bf16[64,24,32,48]{3,1,2,0:T(8,128)(2,1)} copy(bf16[64,24,32,48]{0,3,2,1:T(8,128)(2,1)} %pad_maximum_fusion.3) | data formatting | bytes 9437184 | tf_op jit(solution)/shard_map/concatenate | solution.py:21
  139.8 9.5 convolution_bitcast_fusion
  149.3 5.3 fusion.71
  154.6 12.4 fusion.86
  168.7 147.5 %all-reduce.3.cloned.1.call-done = f32[64,512]{1,0:T(8,128)} async-done(((f32[64,512]{1,0:T(8,128)}), f32[64,512]{1,0:T(8,128)}) %all-reduce.3.cloned.1.call-update) | async-done | bytes 131088 | tf_op jit(solution)/shard_map/psum | solution.py:72
  329.9 16.5 %collective-permute-done.7 = bf16[64,8,16,32]{0,3,2,1:T(8,128)(2,1)} collective-permute-done((bf16[64,8,16,32]{0,3,2,1:T(8,128)(2,1)S(1)}, bf16[64,8,16,32]{0,3,2,1:T(8,128)(2,1)}, u32[]{:S(2)}, u32[]{:S(2)}) %collective-permute-start.7) | collective-permute-done | bytes 524320 | tf_op jit(solution)/shard_map/ppermute | solution.py:20
  364.2 5.4 copy.110
  371.0 5.8 copy.109
  376.8 5.2 collective-permute-start.8
  381.9 24.3 %collective-permute-done.9 = bf16[64,24,8,32]{0,3,2,1:T(8,128)(2,1)} collective-permute-done((bf16[64,24,8,32]{0,3,2,1:T(8,128)(2,1)}, bf16[64,24,8,32]{0,3,2,1:T(8,128)(2,1)}, u32[]{:S(2)}, u32[]{:S(2)}) %collective-permute-start.9) | collective-permute-done | bytes 786464 | tf_op jit(solution)/shard_map/ppermute | solution.py:20
  406.3 6.3 copy.112
  413.0 6.3 copy.111
  419.3 7.7 pad_maximum_fusion
  427.0 10.7 fusion.265
  437.7 12.2 copy.113
  449.9 5.9 collective-permute-start.10
  455.8 12.4 copy.114
  473.5 11.1 copy.115
  484.6 5.7 collective-permute-done.11
  490.3 11.0 copy.116
  501.3 24.1 %fusion.64 = f32[64,8,32,48]{3,1,2,0:T(8,128)} fusion(bf16[64,24,32,8]{3,1,2,0:T(8,128)(2,1)} %copy.116, bf16[64,24,8,32]{3,1,2,0:T(8,128)(2,1)} %copy.112, bf16[64,8,16,32]{3,1,2,0:T(8,128)(2,1)} %copy.108, bf16[64,8,16,32]{3,1,2,0:T(8,128)(2,1)} %copy-done.3, bf16[64,8,16,32]{3,1,2,0:T(8,128)(2,1)} %copy.106, bf16[64,24,8,32]{3,1,2,0:T(8,128)(2,1)} %copy.111, ...), kind=kOutput, calls=%fused_computation.72 | convolution fusion | flops 259524672 | bytes 7864320 | tf_op jit(solution)/shard_map/dot_general | solution.py:37
  525.5 8.8 copy.117
  534.3 5.7 convolution_bitcast_fusion.2
  545.0 67.6 %psum.29 = f32[]{:T(128)} all-reduce(f32[]{:T(128)} %get-tuple-element.22), channel_id=1, replica_groups=mesh['gx'=8,'gy'=4,'gz'=4] {'gx','gy','gz'}, use_global_device_ids=true, to_apply=%region_2.3 | all-reduce | flops 1 | bytes 8 | tf_op jit(solution)/shard_map/psum | solution.py:80
  635.7 16.3 %collective-permute-done.13 = bf16[64,8,16,32]{0,3,2,1:T(8,128)(2,1)} collective-permute-done((bf16[64,8,16,32]{0,3,2,1:T(8,128)(2,1)S(1)}, bf16[64,8,16,32]{0,3,2,1:T(8,128)(2,1)}, u32[]{:S(2)}, u32[]{:S(2)}) %collective-permute-start.13) | collective-permute-done | bytes 524320 | tf_op jit(solution)/shard_map/ppermute | solution.py:20
  669.9 5.4 copy.126
  676.6 5.4 copy.125
  687.2 24.8 %collective-permute-done.15 = bf16[64,24,8,32]{0,3,2,1:T(8,128)(2,1)} collective-permute-done((bf16[64,24,8,32]{0,3,2,1:T(8,128)(2,1)}, bf16[64,24,8,32]{0,3,2,1:T(8,128)(2,1)}, u32[]{:S(2)}, u32[]{:S(2)}) %collective-permute-start.15) | collective-permute-done | bytes 786464 | tf_op jit(solution)/shard_map/ppermute | solution.py:20
  711.9 6.8 copy.128
  718.7 6.4 copy.127
  725.1 7.7 pad_maximum_fusion.1
  732.8 10.7 fusion.264
  743.5 12.2 copy.129
  760.5 12.3 copy.130
  778.2 11.0 copy.131
  789.1 5.7 collective-permute-done.17
  794.8 11.0 copy.132
  805.9 22.3 %fusion.61 = f32[64,8,32,48]{3,1,2,0:T(8,128)S(1)} fusion(bf16[64,24,32,8]{3,1,2,0:T(8,128)(2,1)} %copy.132, bf16[64,24,8,32]{3,1,2,0:T(8,128)(2,1)} %copy.128, bf16[64,8,16,32]{3,1,2,0:T(8,128)(2,1)} %copy.124, bf16[64,8,16,32]{3,1,2,0:T(8,128)(2,1)S(1)} %copy.123, bf16[64,8,16,32]{3,1,2,0:T(8,128)(2,1)} %copy.122, bf16[64,24,8,32]{3,1,2,0:T(8,128)(2,1)} %copy.127, ...), kind=kOutput, calls=%fused_computation.71 | convolution fusion | flops 259524672 | bytes 7864320 | tf_op jit(solution)/shard_map/dot_general | solution.py:37
  828.2 5.3 fusion.74
  833.5 12.4 fusion.83
  847.4 142.3 %all-reduce.5.cloned.1.call-done = f32[64,512]{1,0:T(8,128)} async-done(((f32[64,512]{1,0:T(8,128)}), f32[64,512]{1,0:T(8,128)}) %all-reduce.5.cloned.1.call-update) | async-done | bytes 131088 | tf_op jit(solution)/shard_map/psum | solution.py:72
  1004.3 16.5 %collective-permute-done.19 = bf16[64,8,16,32]{0,3,2,1:T(8,128)(2,1)} collective-permute-done((bf16[64,8,16,32]{0,3,2,1:T(8,128)(2,1)S(1)}, bf16[64,8,16,32]{0,3,2,1:T(8,128)(2,1)}, u32[]{:S(2)}, u32[]{:S(2)}) %collective-permute-start.19) | collective-permute-done | bytes 524320 | tf_op jit(solution)/shard_map/ppermute | solution.py:20
  1038.7 5.4 copy.140
  1045.4 5.8 copy.139
  1056.4 24.3 %collective-permute-done.21 = bf16[64,24,8,32]{0,3,2,1:T(8,128)(2,1)} collective-permute-done((bf16[64,24,8,32]{0,3,2,1:T(8,128)(2,1)}, bf16[64,24,8,32]{0,3,2,1:T(8,128)(2,1)}, u32[]{:S(2)}, u32[]{:S(2)}) %collective-permute-start.21) | collective-permute-done | bytes 786464 | tf_op jit(solution)/shard_map/ppermute | solution.py:20
  1080.7 6.3 copy.142
  1087.4 6.3 copy.141
  1093.7 7.7 pad_maximum_fusion.2
  1101.4 10.7 fusion.263
  1112.1 12.2 copy.143
  1124.3 5.9 collective-permute-start.22
  1130.3 12.3 copy.144
  1147.9 11.1 copy.145
  1159.0 5.6 collective-permute-done.23
  1164.6 11.0 copy.146
  1175.6 24.0 %fusion.58 = f32[64,8,32,48]{3,1,2,0:T(8,128)} fusion(bf16[64,24,32,8]{3,1,2,0:T(8,128)(2,1)} %copy.146, bf16[64,24,8,32]{3,1,2,0:T(8,128)(2,1)} %copy.142, bf16[64,8,16,32]{3,1,2,0:T(8,128)(2,1)} %copy.138, bf16[64,8,16,32]{3,1,2,0:T(8,128)(2,1)S(1)} %copy.137, bf16[64,8,16,32]{3,1,2,0:T(8,128)(2,1)} %copy.136, bf16[64,24,8,32]{3,1,2,0:T(8,128)(2,1)} %copy.141, ...), kind=kOutput, calls=%fused_computation.70 | convolution fusion | flops 259524672 | bytes 7864320 | tf_op jit(solution)/shard_map/dot_general | solution.py:37
  1199.6 8.8 copy.147
  1208.5 5.7 convolution_bitcast_fusion.1
  1218.1 67.6 %psum.31 = f32[]{:T(128)} all-reduce(f32[]{:T(128)} %get-tuple-element.28), channel_id=1, replica_groups=mesh['gx'=8,'gy'=4,'gz'=4] {'gx','gy','gz'}, use_global_device_ids=true, to_apply=%region_6.7 | all-reduce | flops 1 | bytes 8 | tf_op jit(solution)/shard_map/psum | solution.py:80
  (103 shorter events, 187.2 us)
Async XLA Ops:
  7.2 309.1 %all-reduce.3.cloned.1.call-start = ((), (), s32[]{:S(2)}) async-start(), calls=%async_computation | async-start | bytes 262144 | tf_op jit(solution)/shard_map/psum | solution.py:72
  9.0 26.5 %collective-permute-start.1 = (bf16[64,8,16,32]{0,3,2,1:T(8,128)(2,1)S(1)}, bf16[64,8,16,32]{0,3,2,1:T(8,128)(2,1)S(1)}, u32[]{:S(2)}, u32[]{:S(2)}) collective-permute-start(bf16[64,8,16,32]{0,3,2,1:T(8,128)(2,1)S(1)} %convert_element_type.83), channel_id=1, source_target_pairs={{16,0},{32,16},{48,32},{64,48},{80,64},{96,80},{112,96},{17,1},{33... | collective-permute-start | bytes 1572872 | tf_op jit(solution)/shard_map/ppermute | solution.py:20
  10.3 26.2 %collective-permute-start = (bf16[64,8,16,32]{0,3,2,1:T(8,128)(2,1)S(1)}, bf16[64,8,16,32]{0,3,2,1:T(8,128)(2,1)S(1)}, u32[]{:S(2)}, u32[]{:S(2)}) collective-permute-start(bf16[64,8,16,32]{0,3,2,1:T(8,128)(2,1)S(1)} %convert_element_type.83), channel_id=1, source_target_pairs={{0,16},{16,32},{32,48},{48,64},{64,80},{80,96},{96,112},{1,17},{17... | collective-permute-start | bytes 1572872 | tf_op jit(solution)/shard_map/ppermute | solution.py:19
  37.9 35.3 %collective-permute-start.2 = (bf16[64,24,8,32]{0,3,2,1:T(8,128)(2,1)S(1)}, bf16[64,24,8,32]{0,3,2,1:T(8,128)(2,1)S(1)}, u32[]{:S(2)}, u32[]{:S(2)}) collective-permute-start(bf16[64,24,8,32]{0,3,2,1:T(8,128)(2,1)S(1)} %get-tuple-element.18), channel_id=1, source_target_pairs={{0,4},{4,8},{8,12},{1,5},{5,9},{9,13},{2,6},{6,10},{10,14},{3,7},{... | collective-permute-start | bytes 2359304 | tf_op jit(solution)/shard_map/ppermute | solution.py:19
  41.3 35.8 %collective-permute-start.3 = (bf16[64,24,8,32]{0,3,2,1:T(8,128)(2,1)S(1)}, bf16[64,24,8,32]{0,3,2,1:T(8,128)(2,1)S(1)}, u32[]{:S(2)}, u32[]{:S(2)}) collective-permute-start(bf16[64,24,8,32]{0,3,2,1:T(8,128)(2,1)S(1)} %get-tuple-element.19), channel_id=1, source_target_pairs={{4,0},{8,4},{12,8},{5,1},{9,5},{13,9},{6,2},{10,6},{14,10},{7,3},{... | collective-permute-start | bytes 2359304 | tf_op jit(solution)/shard_map/ppermute | solution.py:20
  81.7 23.7 %collective-permute-start.4 = (bf16[64,24,32,8]{0,3,2,1:T(8,128)(2,1)S(1)}, bf16[64,24,32,8]{0,3,2,1:T(8,128)(2,1)S(1)}, u32[]{:S(2)}, u32[]{:S(2)}) collective-permute-start(bf16[64,24,32,8]{0,3,2,1:T(8,128)(2,1)S(1)} %get-tuple-element.16), channel_id=1, source_target_pairs={{0,1},{1,2},{2,3},{4,5},{5,6},{6,7},{8,9},{9,10},{10,11},{12,13},{... | collective-permute-start | bytes 2359304 | tf_op jit(solution)/shard_map/ppermute | solution.py:19
  88.1 21.7 %collective-permute-start.5 = (bf16[64,24,32,8]{0,3,2,1:T(8,128)(2,1)S(1)}, bf16[64,24,32,8]{0,3,2,1:T(8,128)(2,1)S(1)}, u32[]{:S(2)}, u32[]{:S(2)}) collective-permute-start(bf16[64,24,32,8]{0,3,2,1:T(8,128)(2,1)S(1)} %get-tuple-element.17), channel_id=1, source_target_pairs={{1,0},{2,1},{3,2},{5,4},{6,5},{7,6},{9,8},{10,9},{11,10},{13,12},{... | collective-permute-start | bytes 2359304 | tf_op jit(solution)/shard_map/ppermute | solution.py:20
  90.8 63.8 %copy-start.10 = (bf16[8,16]{1,0:T(8,128)(2,1)}, bf16[8,16]{1,0:T(8,128)(2,1)S(1)}, u32[]{:S(2)}) copy-start(bf16[8,16]{1,0:T(8,128)(2,1)S(1)} %get-tuple-element.20) | copy-start | bytes 772
  149.3 17.7 %copy-start = (bf16[8,16,32,512]{3,2,1,0:T(8,128)(2,1)S(1)}, bf16[8,16,32,512]{3,2,1,0:T(8,128)(2,1)}, u32[]{:S(2)}) copy-start(bf16[8,16,32,512]{3,2,1,0:T(8,128)(2,1)} %param.3) | copy-start | bytes 12582916
  168.5 821.2 %all-reduce.5.cloned.1.call-start = ((), (), s32[]{:S(2)}) async-start(), calls=%async_computation.1 | async-start | bytes 262144 | tf_op jit(solution)/shard_map/psum | solution.py:72
  168.7 152.9 %copy-start.8 = (f32[4096]{0:T(1024)}, f32[4096]{0:T(1024)S(1)}, u32[]{:S(2)}) copy-start(f32[4096]{0:T(1024)S(1)} %convert_element_type.91) | copy-start | bytes 49156
  320.4 26.0 %collective-permute-start.7 = (bf16[64,8,16,32]{0,3,2,1:T(8,128)(2,1)S(1)}, bf16[64,8,16,32]{0,3,2,1:T(8,128)(2,1)}, u32[]{:S(2)}, u32[]{:S(2)}) collective-permute-start(bf16[64,8,16,32]{0,3,2,1:T(8,128)(2,1)S(1)} %bitcast.86), channel_id=1, source_target_pairs={{16,0},{32,16},{48,32},{64,48},{80,64},{96,80},{112,96},{17,1},{33... | collective-permute-start | bytes 1572872 | tf_op jit(solution)/shard_map/ppermute | solution.py:20
  321.7 29.5 %collective-permute-start.6 = (bf16[64,8,16,32]{0,3,2,1:T(8,128)(2,1)S(1)}, bf16[64,8,16,32]{0,3,2,1:T(8,128)(2,1)}, u32[]{:S(2)}, u32[]{:S(2)}) collective-permute-start(bf16[64,8,16,32]{0,3,2,1:T(8,128)(2,1)S(1)} %bitcast.87), channel_id=1, source_target_pairs={{0,16},{16,32},{32,48},{48,64},{64,80},{80,96},{96,112},{1,17},{17... | collective-permute-start | bytes 1572872 | tf_op jit(solution)/shard_map/ppermute | solution.py:19
  329.9 89.4 %copy-start.3 = (bf16[64,8,16,32]{3,1,2,0:T(8,128)(2,1)}, bf16[64,8,16,32]{3,1,2,0:T(8,128)(2,1)S(1)}, u32[]{:S(2)}) copy-start(bf16[64,8,16,32]{3,1,2,0:T(8,128)(2,1)S(1)} %copy.107) | copy-start | bytes 1572868
  369.7 36.6 %collective-permute-start.9 = (bf16[64,24,8,32]{0,3,2,1:T(8,128)(2,1)}, bf16[64,24,8,32]{0,3,2,1:T(8,128)(2,1)}, u32[]{:S(2)}, u32[]{:S(2)}) collective-permute-start(bf16[64,24,8,32]{0,3,2,1:T(8,128)(2,1)} %copy.110), channel_id=1, source_target_pairs={{4,0},{8,4},{12,8},{5,1},{9,5},{13,9},{6,2},{10,6},{14,10},{7,3},{... | collective-permute-start | bytes 2359304 | tf_op jit(solution)/shard_map/ppermute | solution.py:20
  376.8 36.2 %collective-permute-start.8 = (bf16[64,24,8,32]{0,3,2,1:T(8,128)(2,1)}, bf16[64,24,8,32]{0,3,2,1:T(8,128)(2,1)}, u32[]{:S(2)}, u32[]{:S(2)}) collective-permute-start(bf16[64,24,8,32]{0,3,2,1:T(8,128)(2,1)} %copy.109), channel_id=1, source_target_pairs={{0,4},{4,8},{8,12},{1,5},{5,9},{9,13},{2,6},{6,10},{10,14},{3,7},{... | collective-permute-start | bytes 2359304 | tf_op jit(solution)/shard_map/ppermute | solution.py:19
  449.9 23.6 %collective-permute-start.10 = (bf16[64,24,32,8]{0,3,2,1:T(8,128)(2,1)}, bf16[64,24,32,8]{0,3,2,1:T(8,128)(2,1)}, u32[]{:S(2)}, u32[]{:S(2)}) collective-permute-start(bf16[64,24,32,8]{0,3,2,1:T(8,128)(2,1)} %copy.113), channel_id=1, source_target_pairs={{0,1},{1,2},{2,3},{4,5},{5,6},{6,7},{8,9},{9,10},{10,11},{12,13},{... | collective-permute-start | bytes 2359304 | tf_op jit(solution)/shard_map/ppermute | solution.py:19
  455.8 14.4 %copy-start.2 = (f32[64,8,16,32]{0,3,2,1:T(8,128)S(1)}, f32[64,8,16,32]{0,3,2,1:T(8,128)}, u32[]{:S(2)}) copy-start(f32[64,8,16,32]{0,3,2,1:T(8,128)} %param.4) | copy-start | bytes 3145732
  455.8 15.0 %copy-start.5 = (f32[64,512]{1,0:T(8,128)S(1)}, f32[64,512]{1,0:T(8,128)}, u32[]{:S(2)}) copy-start(f32[64,512]{1,0:T(8,128)} %all-reduce.3.cloned.1.call-done) | copy-start | bytes 393220
  468.3 22.0 %collective-permute-start.11 = (bf16[64,24,32,8]{0,3,2,1:T(8,128)(2,1)}, bf16[64,24,32,8]{0,3,2,1:T(8,128)(2,1)}, u32[]{:S(2)}, u32[]{:S(2)}) collective-permute-start(bf16[64,24,32,8]{0,3,2,1:T(8,128)(2,1)} %copy.114), channel_id=1, source_target_pairs={{1,0},{2,1},{3,2},{5,4},{6,5},{7,6},{9,8},{10,9},{11,10},{13,12},{... | collective-permute-start | bytes 2359304 | tf_op jit(solution)/shard_map/ppermute | solution.py:20
  625.9 26.1 %collective-permute-start.13 = (bf16[64,8,16,32]{0,3,2,1:T(8,128)(2,1)S(1)}, bf16[64,8,16,32]{0,3,2,1:T(8,128)(2,1)}, u32[]{:S(2)}, u32[]{:S(2)}) collective-permute-start(bf16[64,8,16,32]{0,3,2,1:T(8,128)(2,1)S(1)} %bitcast.89), channel_id=1, source_target_pairs={{16,0},{32,16},{48,32},{64,48},{80,64},{96,80},{112,96},{17,1},{33... | collective-permute-start | bytes 1572872 | tf_op jit(solution)/shard_map/ppermute | solution.py:20
  627.2 29.6 %collective-permute-start.12 = (bf16[64,8,16,32]{0,3,2,1:T(8,128)(2,1)S(1)}, bf16[64,8,16,32]{0,3,2,1:T(8,128)(2,1)}, u32[]{:S(2)}, u32[]{:S(2)}) collective-permute-start(bf16[64,8,16,32]{0,3,2,1:T(8,128)(2,1)S(1)} %bitcast.90), channel_id=1, source_target_pairs={{0,16},{16,32},{32,48},{48,64},{64,80},{80,96},{96,112},{1,17},{17... | collective-permute-start | bytes 1572872 | tf_op jit(solution)/shard_map/ppermute | solution.py:19
  675.3 36.7 %collective-permute-start.15 = (bf16[64,24,8,32]{0,3,2,1:T(8,128)(2,1)}, bf16[64,24,8,32]{0,3,2,1:T(8,128)(2,1)}, u32[]{:S(2)}, u32[]{:S(2)}) collective-permute-start(bf16[64,24,8,32]{0,3,2,1:T(8,128)(2,1)} %copy.126), channel_id=1, source_target_pairs={{4,0},{8,4},{12,8},{5,1},{9,5},{13,9},{6,2},{10,6},{14,10},{7,3},{... | collective-permute-start | bytes 2359304 | tf_op jit(solution)/shard_map/ppermute | solution.py:20
  682.0 36.7 %collective-permute-start.14 = (bf16[64,24,8,32]{0,3,2,1:T(8,128)(2,1)}, bf16[64,24,8,32]{0,3,2,1:T(8,128)(2,1)}, u32[]{:S(2)}, u32[]{:S(2)}) collective-permute-start(bf16[64,24,8,32]{0,3,2,1:T(8,128)(2,1)} %copy.125), channel_id=1, source_target_pairs={{0,4},{4,8},{8,12},{1,5},{5,9},{9,13},{2,6},{6,10},{10,14},{3,7},{... | collective-permute-start | bytes 2359304 | tf_op jit(solution)/shard_map/ppermute | solution.py:19
  755.7 22.5 %collective-permute-start.16 = (bf16[64,24,32,8]{0,3,2,1:T(8,128)(2,1)}, bf16[64,24,32,8]{0,3,2,1:T(8,128)(2,1)}, u32[]{:S(2)}, u32[]{:S(2)}) collective-permute-start(bf16[64,24,32,8]{0,3,2,1:T(8,128)(2,1)} %copy.129), channel_id=1, source_target_pairs={{0,1},{1,2},{2,3},{4,5},{5,6},{6,7},{8,9},{9,10},{10,11},{12,13},{... | collective-permute-start | bytes 2359304 | tf_op jit(solution)/shard_map/ppermute | solution.py:19
  772.8 22.0 %collective-permute-start.17 = (bf16[64,24,32,8]{0,3,2,1:T(8,128)(2,1)}, bf16[64,24,32,8]{0,3,2,1:T(8,128)(2,1)}, u32[]{:S(2)}, u32[]{:S(2)}) collective-permute-start(bf16[64,24,32,8]{0,3,2,1:T(8,128)(2,1)} %copy.130), channel_id=1, source_target_pairs={{1,0},{2,1},{3,2},{5,4},{6,5},{7,6},{9,8},{10,9},{11,10},{13,12},{... | collective-permute-start | bytes 2359304 | tf_op jit(solution)/shard_map/ppermute | solution.py:20
  828.2 5.3 copy-start.11
  828.2 17.7 %copy-start.1 = (bf16[8,16,32,512]{3,2,1,0:T(8,128)(2,1)S(1)}, bf16[8,16,32,512]{3,2,1,0:T(8,128)(2,1)}, u32[]{:S(2)}) copy-start(bf16[8,16,32,512]{3,2,1,0:T(8,128)(2,1)} %param.3) | copy-start | bytes 12582916
  833.5 157.2 %copy-start.9 = (f32[4096]{0:T(1024)S(1)}, f32[4096]{0:T(1024)}, u32[]{:S(2)}) copy-start(f32[4096]{0:T(1024)} %copy-done.8) | copy-start | bytes 49156
  990.7 34.9 %copy-start.7 = (bf16[64,512]{1,0:T(8,128)(2,1)}, bf16[64,512]{1,0:T(8,128)(2,1)S(1)}, u32[]{:S(2)}) copy-start(bf16[64,512]{1,0:T(8,128)(2,1)S(1)} %convert_element_type.96) | copy-start | bytes 196612
  994.8 26.0 %collective-permute-start.19 = (bf16[64,8,16,32]{0,3,2,1:T(8,128)(2,1)S(1)}, bf16[64,8,16,32]{0,3,2,1:T(8,128)(2,1)}, u32[]{:S(2)}, u32[]{:S(2)}) collective-permute-start(bf16[64,8,16,32]{0,3,2,1:T(8,128)(2,1)S(1)} %bitcast.92), channel_id=1, source_target_pairs={{16,0},{32,16},{48,32},{64,48},{80,64},{96,80},{112,96},{17,1},{33... | collective-permute-start | bytes 1572872 | tf_op jit(solution)/shard_map/ppermute | solution.py:20
  996.1 29.6 %collective-permute-start.18 = (bf16[64,8,16,32]{0,3,2,1:T(8,128)(2,1)S(1)}, bf16[64,8,16,32]{0,3,2,1:T(8,128)(2,1)}, u32[]{:S(2)}, u32[]{:S(2)}) collective-permute-start(bf16[64,8,16,32]{0,3,2,1:T(8,128)(2,1)S(1)} %bitcast.93), channel_id=1, source_target_pairs={{0,16},{16,32},{32,48},{48,64},{64,80},{80,96},{96,112},{1,17},{17... | collective-permute-start | bytes 1572872 | tf_op jit(solution)/shard_map/ppermute | solution.py:19
  1044.1 36.6 %collective-permute-start.21 = (bf16[64,24,8,32]{0,3,2,1:T(8,128)(2,1)}, bf16[64,24,8,32]{0,3,2,1:T(8,128)(2,1)}, u32[]{:S(2)}, u32[]{:S(2)}) collective-permute-start(bf16[64,24,8,32]{0,3,2,1:T(8,128)(2,1)} %copy.140), channel_id=1, source_target_pairs={{4,0},{8,4},{12,8},{5,1},{9,5},{13,9},{6,2},{10,6},{14,10},{7,3},{... | collective-permute-start | bytes 2359304 | tf_op jit(solution)/shard_map/ppermute | solution.py:20
  1051.2 36.2 %collective-permute-start.20 = (bf16[64,24,8,32]{0,3,2,1:T(8,128)(2,1)}, bf16[64,24,8,32]{0,3,2,1:T(8,128)(2,1)}, u32[]{:S(2)}, u32[]{:S(2)}) collective-permute-start(bf16[64,24,8,32]{0,3,2,1:T(8,128)(2,1)} %copy.139), channel_id=1, source_target_pairs={{0,4},{4,8},{8,12},{1,5},{5,9},{9,13},{2,6},{6,10},{10,14},{3,7},{... | collective-permute-start | bytes 2359304 | tf_op jit(solution)/shard_map/ppermute | solution.py:19
  1124.3 23.6 %collective-permute-start.22 = (bf16[64,24,32,8]{0,3,2,1:T(8,128)(2,1)}, bf16[64,24,32,8]{0,3,2,1:T(8,128)(2,1)}, u32[]{:S(2)}, u32[]{:S(2)}) collective-permute-start(bf16[64,24,32,8]{0,3,2,1:T(8,128)(2,1)} %copy.143), channel_id=1, source_target_pairs={{0,1},{1,2},{2,3},{4,5},{5,6},{6,7},{8,9},{9,10},{10,11},{12,13},{... | collective-permute-start | bytes 2359304 | tf_op jit(solution)/shard_map/ppermute | solution.py:19
  1130.2 14.2 %copy-start.6 = (f32[64,512]{1,0:T(8,128)S(1)}, f32[64,512]{1,0:T(8,128)}, u32[]{:S(2)}) copy-start(f32[64,512]{1,0:T(8,128)} %all-reduce.5.cloned.1.call-done) | copy-start | bytes 393220
  1142.6 22.0 %collective-permute-start.23 = (bf16[64,24,32,8]{0,3,2,1:T(8,128)(2,1)}, bf16[64,24,32,8]{0,3,2,1:T(8,128)(2,1)}, u32[]{:S(2)}, u32[]{:S(2)}) collective-permute-start(bf16[64,24,32,8]{0,3,2,1:T(8,128)(2,1)} %copy.144), channel_id=1, source_target_pairs={{1,0},{2,1},{3,2},{5,4},{6,5},{7,6},{9,8},{10,9},{11,10},{13,12},{... | collective-permute-start | bytes 2359304 | tf_op jit(solution)/shard_map/ppermute | solution.py:20
  1214.2 76.0 %copy-start.4 = (f32[64,4096]{1,0:T(8,128)S(1)}, f32[64,4096]{1,0:T(8,128)}, u32[]{:S(2)}) copy-start(f32[64,4096]{1,0:T(8,128)} %get-tuple-element.27) | copy-start | bytes 3145732
Sparse Core Ops, SparseCore 0:
  168.6 147.5 all-reduce.2
  847.5 142.1 all-reduce.4
where the time goes:
time: 1310 us; the launch traced here: 1300 us
  waiting for transfers between devices  512 us (39%)
  local copies, waits for them, and re-layouts  341 us (26%)
  matrix products  153 us (12%)
  blocking collectives  135 us (10%)
  starting transfers between devices  79.6 us (6%)
  other arithmetic  61 us (5%)
  between operations  18.1 us (1%)
    psum x2, waiting for transfers between devices, per_device(): courses = lax.psum(partial_courses, ('gx', 'gy', 'gz'))  290 us
    ppermute x12, waiting for transfers between devices, extended(): after = lax.ppermute(leading, axis, down)  169 us
    dot_general x12, matrix products, filter_along(): jnp.tensordot(field, band, axes=((axis,), (0,)), precision=lax.Precision....  135 us
    psum x2, blocking collectives, per_device(): energy = lax.psum(jnp.sum(grad * grad), ('gx', 'gy', 'gz')) / all_cells  135 us
    slice x13, local copies, waits for them, and re-layouts, extended(): last = lax.slice_in_dim(x, length - width, length, axis=dim)  98.7 us
    ppermute x9, local copies, waits for them, and re-layouts, extended(): before = lax.ppermute(last, axis, up)  67.1 us
    ppermute x9, local copies, waits for them, and re-layouts, extended(): after = lax.ppermute(leading, axis, down)  67 us
    ppermute x12, starting transfers between devices, extended(): before = lax.ppermute(last, axis, up)  61.5 us
  transfers between devices with their start and end apart: 26, of which 22 were waited for; matrix products, arithmetic and copies ran while one was open for 10% of the time, Pallas kernels for 0%

commit v1 on v0

v1 whole, which is shorter than its diff:
```python
import functools
import math

import jax
import jax.numpy as jnp
import numpy as np
from jax import lax
from jax.experimental import pallas as pl
from jax.experimental.pallas import tpu as pltpu
from jax.sharding import PartitionSpec as P

MESH = pl.DeviceIdType.MESH
RADIUS = 8
K, T = 64, 512
BX, BY, BZ = 8, 16, 32
YZ = BY * BZ
CH = 16
NC = K // CH
ROWS = BX * CH
F32, BF16 = jnp.float32, jnp.bfloat16
HIGH = lax.Precision.HIGHEST


def tap_of(offset):
    total = sum(math.exp(-float(d * d) / 32.0) for d in range(-RADIUS, RADIUS + 1))
    taps = np.exp(-np.square(np.asarray(offset, np.float64)) / 32.0) / total
    return np.where(np.abs(offset) <= RADIUS, taps, 0.0)


def filter_matrices():
    col = np.arange(YZ)
    col_y, col_z = col // BZ, col % BZ
    edge = np.arange(2 * BY * RADIUS)
    edge_y = (edge % (BY * RADIUS)) // RADIUS
    low = edge < BY * RADIUS
    edge_z = np.where(low, edge % RADIUS, BZ - RADIUS + edge % RADIUS)
    pack = (col_y[:, None] == edge_y[None]) & (col_z[:, None] == edge_z[None])
    half_y, half_z = col_y[: YZ // 2], col_z[: YZ // 2]
    own_z = (half_y[:, None] == half_y[None]) * tap_of(half_z[:, None] - half_z[None])
    from_z = np.where(low, edge % RADIUS - RADIUS, BZ + edge % RADIUS)
    edges_z = (edge_y[:, None] == col_y[None]) * tap_of(from_z[:, None] - col_z[None])
    row = np.arange(2 * YZ)
    row_y = np.where(row < YZ, row // BZ, np.where(row < YZ * 3 // 2, (row - YZ) // BZ - RADIUS, (row - YZ) // BZ - RADIUS + BY))
    full_y = ((row % BZ)[:, None] == col_z[None]) * tap_of(row_y[:, None] - col_y[None])
    out = np.arange(ROWS)
    src = np.arange(3 * ROWS)
    full_x = ((src % CH)[None] == (out % CH)[:, None]) * tap_of((src // CH - BX)[None] - (out // CH)[:, None])
    return [jnp.asarray(m, BF16) for m in (pack, own_z, edges_z, full_y, full_x)]


def kernel(
    nx, ny, nz,
    live_ref, plain_hbm, w_hbm, x_hbm, pack_hbm, ownz_hbm, edgez_hbm, fully_hbm, fullx_hbm,
    out_ref, tc_ref,
    src, wmap, xdat, pack, ownz, edgez, fully, fullx,
    zpack, fz, fyz, smooth, ze, ye, xe, grad, mixed,
    cpart, c1, c2, rz, ry, rx, etot, ez, ey, ex,
    load_sem, hs, hr, az_s, az_r, ay_s, ay_r, ax_s, ax_r, gy_s, gy_r, gz_s, gz_r,
    es_z, er_z, es_y, er_y, es_x, er_x,
):
    ix, iy, iz = lax.axis_index("gx"), lax.axis_index("gy"), lax.axis_index("gz")
    rows_z, lanes_y = K // nz, T // ny
    cells = float(K * BX * BY * BZ * nx * ny * nz)

    loads = [
        pltpu.make_async_copy(a, b, load_sem.at[i])
        for i, (a, b) in enumerate(
            [(plain_hbm, src), (pack_hbm, pack), (ownz_hbm, ownz), (edgez_hbm, edgez), (fully_hbm, fully),
             (fullx_hbm, fullx), (x_hbm, xdat), (w_hbm, wmap)]
        )
    ]
    for load in loads:
        load.start()

    barrier = pltpu.get_barrier_semaphore()
    for name, me, n in (("gx", ix, nx), ("gy", iy, ny), ("gz", iz, nz)):
        for d in range(1, n):
            pl.semaphore_signal(barrier, inc=1, device_id={name: lax.rem(me + d, n)}, device_id_type=MESH)

    @pl.when(ix == 0)
    def _():
        xe[:, 0] = jnp.zeros_like(xe[:, 0])

    @pl.when(ix == nx - 1)
    def _():
        xe[:, 1] = jnp.zeros_like(xe[:, 1])

    @pl.when(iy == 0)
    def _():
        ye[:, :, :, : YZ // 2] = jnp.zeros_like(ye[:, :, :, : YZ // 2])

    @pl.when(iy == ny - 1)
    def _():
        ye[:, :, :, YZ // 2 :] = jnp.zeros_like(ye[:, :, :, YZ // 2 :])

    @pl.when(iz == 0)
    def _():
        ze[:, :, :, :128] = jnp.zeros_like(ze[:, :, :, :128])

    @pl.when(iz == nz - 1)
    def _():
        ze[:, :, :, 128:] = jnp.zeros_like(ze[:, :, :, 128:])

    pl.semaphore_wait(barrier, nx + ny + nz - 3)
    loads[0].wait()
    loads[1].wait()

    def dot(a, b):
        return jnp.dot(a, b, preferred_element_type=F32)

    def maps(c):
        return pl.ds(pl.multiple_of(c * CH, CH), CH)

    def halo(s, c, axis):
        k = maps(c)

        def copy(i, a, b, axis, to):
            return pltpu.make_async_remote_copy(
                src_ref=a, dst_ref=b, send_sem=hs.at[s, c, i], recv_sem=hr.at[s, c, i],
                device_id={axis: to}, device_id_type=MESH,
            )

        half = YZ // 2
        if axis == "z":
            down = (0, zpack.at[:, k, pl.ds(0, 128)], ze.at[s, :, k, pl.ds(128, 128)])
            up = (1, zpack.at[:, k, pl.ds(128, 128)], ze.at[s, :, k, pl.ds(0, 128)])
            name, me, n = "gz", iz, nz
        elif axis == "y":
            down = (2, fz.at[:, k, pl.ds(0, half)], ye.at[s, :, k, pl.ds(half, half)])
            up = (3, fz.at[:, k, pl.ds(half, half)], ye.at[s, :, k, pl.ds(0, half)])
            name, me, n = "gy", iy, ny
        else:
            down = (4, fyz.at[:, k, :], xe.at[s, 1, :, k, :])
            up = (5, fyz.at[:, k, :], xe.at[s, 0, :, k, :])
            name, me, n = "gx", ix, nx
        return (
            (me > 0, me < n - 1, copy(*down, name, lax.rem(me + n - 1, n))),
            (me < n - 1, me > 0, copy(*up, name, lax.rem(me + 1, n))),
        )

    def send(s, c, axis):
        for sends, _, copy in halo(s, c, axis):
            @pl.when(sends)
            def _():
                copy.start()

    def receive(s, c, axis):
        for _, comes, copy in halo(s, c, axis):
            @pl.when(comes)
            def _():
                copy.wait_recv()

    def sent(s, c):
        for axis in "zyx":
            for sends, _, copy in halo(s, c, axis):
                @pl.when(sends)
                def _():
                    copy.wait_send()

    count = live_ref[0, 0, 0]
    row_y = lax.broadcasted_iota(jnp.int32, (1, YZ), 1) // BZ

    def chunks(body):
        lax.fori_loop(0, NC, lambda c, _: (body(c), 0)[1], 0)

    def smoothing(s, finish):
        def pack_z(c):
            k = maps(c)
            zpack[:, k, :] = dot(src[:, k, :].reshape(ROWS, YZ), pack[...]).astype(BF16).reshape(BX, CH, 2 * 128)
            send(s, c, "z")

        def filter_z(c):
            k = maps(c)
            receive(s, c, "z")
            field = src[:, k, :].reshape(ROWS, YZ)
            own = jnp.concatenate([dot(field[:, : YZ // 2], ownz[...]), dot(field[:, YZ // 2 :], ownz[...])], axis=1)
            edges = dot(ze[s, :, k, :].reshape(ROWS, 2 * 128), edgez[...])
            fz[:, k, :] = (own + edges).astype(BF16).reshape(BX, CH, YZ)
            send(s, c, "y")

        def filter_y(c):
            k = maps(c)
            receive(s, c, "y")
            field = jnp.concatenate([fz[:, k, :].reshape(ROWS, YZ), ye[s, :, k, :].reshape(ROWS, YZ)], axis=1)
            fyz[:, k, :] = dot(field, fully[...]).astype(BF16).reshape(BX, CH, YZ)
            send(s, c, "x")

        def filter_x(c):
            k = maps(c)
            receive(s, c, "x")
            field = jnp.concatenate(
                [xe[s, 0, :, k, :].reshape(ROWS, YZ), fyz[:, k, :].reshape(ROWS, YZ), xe[s, 1, :, k, :].reshape(ROWS, YZ)],
                axis=0,
            )
            finish(c, dot(fullx[...], field).reshape(BX, CH, YZ))

        chunks(pack_z)
        if s == 0:
            loads[2].wait()
            loads[3].wait()
        chunks(filter_z)
        if s == 0:
            loads[4].wait()
        chunks(filter_y)
        if s == 0:
            loads[5].wait()
        return filter_x

    def end_of(s):
        chunks(lambda c: sent(s, c))

    def mask_of(x):
        return x * BY + row_y < count

    def finish_smooth(c, value):
        k = maps(c)
        for x in range(BX):
            smooth[x, k, :] = jnp.where(mask_of(x), value[x], 0.0).astype(BF16)

    def finish_grad(c, value):
        grad[:, maps(c), :] = value
        src[:, maps(c), :] = value.astype(BF16)

    def finish_last(c, value):
        out_ref[:, maps(c), :] = value

    def square_sum(ref):
        def body(x, total):
            return total + ref[x] * ref[x]

        return jnp.sum(lax.fori_loop(0, BX, body, jnp.zeros((K, YZ), F32)))

    def contribution():
        total = dot(smooth[0], xdat[pl.ds(0, YZ), :])
        for x in range(1, BX):
            total += dot(smooth[x], xdat[pl.ds(x * YZ, YZ), :])
        return total

    def gradient(courses):
        for x in range(BX):
            value = lax.dot_general(
                courses, xdat[pl.ds(x * YZ, YZ), :], (((1,), (1,)), ((), ())), preferred_element_type=F32
            )
            src[x] = jnp.where(mask_of(x), value, 0.0).astype(BF16)

    def remote(a, b, ssem, rsem, axis, to):
        return pltpu.make_async_remote_copy(
            src_ref=a, dst_ref=b, send_sem=ssem, recv_sem=rsem, device_id={axis: to}, device_id_type=MESH
        )

    def swap(axis, me, n, piece, slots, ssem, rsem):
        copies = []
        for d in range(1, n):
            to = lax.rem(me + d, n)
            copy = remote(piece(to), slots.at[me], ssem.at[d - 1], rsem.at[me], axis, to)
            copy.start()
            copies.append(copy)
        for d in range(1, n):
            come = lax.rem(me + d, n)
            remote(piece(come), slots.at[come], ssem.at[d - 1], rsem.at[come], axis, come).wait_recv()
        return copies

    def sum_slots(slots, n):
        total = slots[0]
        for j in range(1, n):
            total += slots[j]
        return total

    def all_reduce(a, extra, result):
        height = rows_z + 8
        copies = swap("gz", iz, nz, lambda j: cpart.at[j], rz.at[a], az_s.at[a], az_r.at[a])
        rz[a, iz] = cpart[iz]
        part = sum_slots(rz.at[a], nz)
        for j in range(ny):
            ry[a, ny + j] = part[:, j * lanes_y : (j + 1) * lanes_y]
        copies += swap("gy", iy, ny, lambda j: ry.at[a, ny + j], ry.at[a], ay_s.at[a], ay_r.at[a])
        ry[a, iy] = ry[a, ny + iy]
        rx[a, nx] = sum_slots(ry.at[a], ny)
        copies += swap("gx", ix, nx, lambda j: rx.at[a, nx], rx.at[a], ax_s.at[a], ax_r.at[a])
        rx[a, ix] = rx[a, nx]
        total = sum_slots(rx.at[a], nx)
        etot[...] = total[rows_z:, :128]
        rows = pl.ds(pl.multiple_of(iz * rows_z, rows_z), rows_z)
        lanes = pl.ds(pl.multiple_of(iy * lanes_y, lanes_y), lanes_y)
        result[rows, lanes] = total[:rows_z]
        for d in range(1, ny):
            to = lax.rem(iy + d, ny)
            copy = remote(result.at[rows, lanes], result.at[rows, lanes], gy_s.at[a, d - 1], gy_r.at[a, iy], "gy", to)
            copy.start()
            copies.append(copy)
        for d in range(1, ny):
            come = lax.rem(iy + d, ny)
            there = result.at[rows, pl.ds(pl.multiple_of(come * lanes_y, lanes_y), lanes_y)]
            remote(there, there, gy_s.at[a, d - 1], gy_r.at[a, come], "gy", come).wait_recv()
        for d in range(1, nz):
            to = lax.rem(iz + d, nz)
            copy = remote(result.at[rows, :], result.at[rows, :], gz_s.at[a, d - 1], gz_r.at[a, iz], "gz", to)
            copy.start()
            copies.append(copy)
        for d in range(1, nz):
            come = lax.rem(iz + d, nz)
            there = result.at[pl.ds(pl.multiple_of(come * rows_z, rows_z), rows_z), :]
            remote(there, there, gz_s.at[a, d - 1], gz_r.at[a, come], "gz", come).wait_recv()
        for copy in copies:
            copy.wait_send()

    def fill_cpart(value, energy):
        for j in range(nz):
            cpart[j, :rows_z] = value[j * rows_z : (j + 1) * rows_z]
            cpart[j, rows_z:] = jnp.full((8, T), energy, F32)

    def gram_of(courses):
        gram = lax.dot_general(courses, courses, (((1,), (1,)), ((), ())), precision=HIGH, preferred_element_type=F32)
        diag = lax.broadcasted_iota(jnp.int32, (K, K), 0) == lax.broadcasted_iota(jnp.int32, (K, K), 1)
        return gram, jnp.sum(jnp.where(diag, gram, 0.0))

    def exact(a, b):
        return jnp.dot(a, b, precision=HIGH, preferred_element_type=F32)

    last = smoothing(0, finish_smooth)
    loads[6].wait()
    chunks(last)
    end_of(0)
    fill_cpart(contribution(), 0.0)
    all_reduce(0, None, c1)
    gradient(c1[...].astype(BF16))
    last = smoothing(1, finish_grad)
    gram1, trace1 = gram_of(c1[...])
    decay1 = float(K) / trace1 * gram1
    loads[7].wait()
    chunks(last)
    end_of(1)
    energy1 = square_sum(grad)
    last = smoothing(2, finish_smooth)
    for x in range(BX):
        mixed[x] = wmap[x] - 0.5 * exact(decay1, wmap[x])
    chunks(last)
    end_of(2)
    fill_cpart(contribution(), energy1)
    all_reduce(1, None, c2)
    scale1 = 1.0 / jnp.sqrt(etot[0:1, 0:1] / cells + 1e-06)
    c2[...] = c1[...] + 0.5 * (scale1 * c2[...] - exact(decay1, c1[...]))
    tc_ref[...] = c2[...].astype(BF16)
    gradient(c2[...].astype(BF16))
    last = smoothing(3, finish_last)
    gram2, trace2 = gram_of(c2[...])
    decay2 = float(K) / trace2 * gram2
    for x in range(BX):
        now = mixed[x] + 0.5 * scale1 * grad[x]
        mixed[x] = now - 0.5 * exact(decay2, now)
    chunks(last)
    end_of(3)
    etot[...] = jnp.full((8, 128), square_sum(out_ref), F32)
    copies = []
    for axis, me, n, slots, ssem, rsem in (
        ("gz", iz, nz, ez, es_z, er_z), ("gy", iy, ny, ey, es_y, er_y), ("gx", ix, nx, ex, es_x, er_x)
    ):
        slots[n] = etot[...]
        copies += swap(axis, me, n, lambda j: slots.at[n], slots, ssem, rsem)
        slots[me] = slots[n]
        etot[...] = sum_slots(slots, n)
    scale2 = 1.0 / jnp.sqrt(etot[0:1, 0:1] / cells + 1e-06)
    for x in range(BX):
        out_ref[x] = mixed[x] + 0.5 * scale2 * out_ref[x]
    for copy in copies:
        copy.wait_send()


def per_device(nx, ny, nz, bold_data, spatial_maps, live_blocks):
    rows_z, lanes_y = K // nz, T // ny
    planes = jnp.transpose(spatial_maps, (1, 0, 2, 3)).reshape(BX, K, YZ)
    matrices = filter_matrices()
    vmem, dma = pltpu.VMEM, pltpu.SemaphoreType.DMA
    field = vmem((BX, K, YZ), BF16)
    new_maps, courses = pl.pallas_call(
        functools.partial(kernel, nx, ny, nz),
        out_shape=(jax.ShapeDtypeStruct((BX, K, YZ), F32), jax.ShapeDtypeStruct((K, T), BF16)),
        in_specs=[pl.BlockSpec(memory_space=pltpu.SMEM)] + [pl.BlockSpec(memory_space=pl.ANY)] * 8,
        out_specs=(pl.BlockSpec(memory_space=pltpu.VMEM), pl.BlockSpec(memory_space=pltpu.VMEM)),
        scratch_shapes=[
            field, vmem((BX, K, YZ), F32), vmem((BX * YZ, T), BF16),
            *[vmem(m.shape, BF16) for m in matrices],
            vmem((BX, K, 256), BF16), field, field, field,
            vmem((4, BX, K, 256), BF16), vmem((4, BX, K, YZ), BF16), vmem((4, 2, BX, K, YZ), BF16),
            vmem((BX, K, YZ), F32), vmem((BX, K, YZ), F32),
            vmem((nz, rows_z + 8, T), F32), vmem((K, T), F32), vmem((K, T), F32),
            vmem((2, nz, rows_z + 8, T), F32),
            vmem((2, 2 * ny, rows_z + 8, lanes_y), F32),
            vmem((2, nx + 1, rows_z + 8, lanes_y), F32),
            vmem((8, 128), F32), vmem((nz + 1, 8, 128), F32), vmem((ny + 1, 8, 128), F32), vmem((nx + 1, 8, 128), F32),
            dma((8,)), dma((4, NC, 6)), dma((4, NC, 6)),
            dma((2, nz)), dma((2, nz)), dma((2, ny)), dma((2, ny)), dma((2, nx)), dma((2, nx)),
            dma((2, ny)), dma((2, ny)), dma((2, nz)), dma((2, nz)),
            dma((nz,)), dma((nz,)), dma((ny,)), dma((ny,)), dma((nx,)), dma((nx,)),
        ],
        compiler_params=pltpu.CompilerParams(
            collective_id=0, has_side_effects=True, vmem_limit_bytes=56 * 1024 * 1024
        ),
    )(live_blocks, planes.astype(BF16), planes, bold_data.reshape(BX * YZ, T), *matrices)
    new_maps = jnp.transpose(new_maps.reshape(BX, K, BY, BZ), (1, 0, 2, 3))
    return new_maps, courses


def solution(mesh):
    return jax.shard_map(
        functools.partial(per_device, mesh.shape["gx"], mesh.shape["gy"], mesh.shape["gz"]),
        mesh=mesh,
        in_specs=(P("gx", "gy", "gz", None), P(None, "gx", "gy", "gz"), P("gx", "gy", "gz")),
        out_specs=(P(None, "gx", "gy", "gz"), P()),
        check_vma=False,
    )
```

time: 1310 us -> 150 us (0.11)
  waiting for transfers between devices: 512 us -> 0 us
  local copies, waits for them, and re-layouts: 341 us -> 6.19 us
  matrix products: 153 us -> 0 us
  Pallas kernels: 0 us -> 141 us
  blocking collectives: 135 us -> 0 us
  starting transfers between devices: 79.6 us -> 0 us
  other arithmetic: 61 us -> 0.94 us
  between operations: 18.1 us -> 1.31 us
    psum x2 -> x0, waiting for transfers between devices: 290 us -> none  [per_device(): courses = lax.psum(partial_courses, ('gx', 'gy', 'gz'))]
    ppermute x24 -> x0, waiting for transfers between devices: 222 us -> none  [the longest x12 169 us: extended(): after = lax.ppermute(leading, axis, down)]
    dot_general x20 -> x0, matrix products: 153 us -> none  [the longest x12 135 us: filter_along(): jnp.tensordot(field, band, axes=((axis,), (0,)), precision=lax.Precision....]
    slice x19 -> x0, local copies, waits for them, and re-layouts: 152 us -> none  [the longest x13 98.7 us: extended(): last = lax.slice_in_dim(x, length - width, length, axis=dim)]
    pallas_call x0 -> x1, Pallas kernels: none -> 141 us  [per_device(): pl.pallas_call(functools.partial(kernel, nx, ny, nz), out_shape=(jax.Shap...]
    psum x2 -> x0, blocking collectives: 135 us -> none  [per_device(): energy = lax.psum(jnp.sum(grad * grad), ('gx', 'gy', 'gz')) / all_cells]
    ppermute x18 -> x0, local copies, waits for them, and re-layouts: 134 us -> none  [the longest x9 67.1 us: extended(): before = lax.ppermute(last, axis, up)]
    ppermute x24 -> x0, starting transfers between devices: 79.5 us -> none  [the longest x12 61.5 us: extended(): before = lax.ppermute(last, axis, up)]
  transfers between devices with their start and end apart: 26 -> 0, of which waited for: 22 -> 0; matrix products, arithmetic and copies ran while one was open for 10% -> 0% of each run, Pallas kernels for 0% -> 0%
where the time goes in v1:
time: 150 us
  Pallas kernels  141 us (94%)
  local copies, waits for them, and re-layouts  6.19 us (4%)
    pallas_call x1, Pallas kernels, per_device(): pl.pallas_call(functools.partial(kernel, nx, ny, nz), out_shape=(jax.Shap...  141 us
    pallas_call x1, local copies, waits for them, and re-layouts, per_device(): pl.pallas_call(functools.partial(kernel, nx, ny, nz), out_shape=(jax.Shap...  3.18 us

profile of v1, /device:TPU:1, one launch (start us, length us, event | category | flops | bytes accessed | tf_op | source)
XLA Modules:
  0.0 149.6 jit_solution(6497173121102995175)
XLA Ops:
  1.3 2.2 %copy.12.w_hbm = f32[8,64,512]{2,1,0:T(8,128)S(1)} copy(f32[8,64,512]{1,2,0:T(8,128)} %bitcast.8) | data formatting | bytes 2097152 | tf_op jit(solution)/shard_map/reshape | solution.py:371
  3.5 0.0 copy-start
  3.5 0.9 convert_element_type.3.plain_hbm
  4.4 0.2 copy-done
  4.6 141.1 %shard_map.95 = (f32[8,64,512]{2,1,0:T(8,128)}, bf16[64,512]{1,0:T(8,128)(2,1)}) custom-call(s32[1,1,1]{2,1,0:T(1,128)S(6)} %copy.16.live_ref, bf16[8,64,512]{2,1,0:T(8,128)(2,1)} %convert_element_type.3.plain_hbm, f32[8,64,512]{2,1,0:T(8,128)} %copy-done, bf16[4096,512]{1,0:T(8,128)(2,1)} %bitcast.7, bf16[512,256]{1,0:T(8,128)(2,1)} %constant.10.clone.pack_hbm, ...), custom_call_target="tpu_custom_call" | custom-call | tf_op jit(solution)/shard_map/pallas_call | solution.py:375
  145.7 0.0 copy-start.1
  145.8 3.2 %copy.14 = f32[8,64,512]{1,2,0:T(8,128)} copy(f32[8,64,512]{2,1,0:T(8,128)} %get-tuple-element.4) | data formatting | bytes 2097152 | tf_op jit(solution)/shard_map/pallas_call | solution.py:375
  148.9 0.0 copy-done.1
  148.9 0.6 copy.17
Async XLA Ops:
  3.5 1.1 copy-start
  145.7 3.2 %copy-start.1 = (bf16[64,512]{1,0:T(8,128)(2,1)S(1)}, bf16[64,512]{1,0:T(8,128)(2,1)}, u32[]{:S(2)}) copy-start(bf16[64,512]{1,0:T(8,128)(2,1)} %get-tuple-element.9) | copy-start | bytes 196612

commit v2 on v0

v2 whole, which is shorter than its diff:
```python
import functools
import math

import jax
import jax.numpy as jnp
import numpy as np
from jax import lax
from jax.experimental import pallas as pl
from jax.experimental.pallas import tpu as pltpu
from jax.sharding import PartitionSpec as P

MESH = pl.DeviceIdType.MESH
RADIUS = 8
K, T = 64, 512
BX, BY, BZ = 8, 16, 32
YZ = BY * BZ
CH = 16
NC = K // CH
PAIR = 2
PR, NP = PAIR * CH, NC // PAIR
ROWS = BX * CH
F32, BF16 = jnp.float32, jnp.bfloat16
HIGH = lax.Precision.HIGHEST


def tap_of(offset):
    total = sum(math.exp(-float(d * d) / 32.0) for d in range(-RADIUS, RADIUS + 1))
    taps = np.exp(-np.square(np.asarray(offset, np.float64)) / 32.0) / total
    return np.where(np.abs(offset) <= RADIUS, taps, 0.0)


def filter_matrices():
    col = np.arange(YZ)
    col_y, col_z = col // BZ, col % BZ
    edge = np.arange(2 * BY * RADIUS)
    edge_y = (edge % (BY * RADIUS)) // RADIUS
    low = edge < BY * RADIUS
    edge_z = np.where(low, edge % RADIUS, BZ - RADIUS + edge % RADIUS)
    pack = (col_y[:, None] == edge_y[None]) & (col_z[:, None] == edge_z[None])
    half_y, half_z = col_y[: YZ // 2], col_z[: YZ // 2]
    own_z = (half_y[:, None] == half_y[None]) * tap_of(half_z[:, None] - half_z[None])
    from_z = np.where(low, edge % RADIUS - RADIUS, BZ + edge % RADIUS)
    edges_z = (edge_y[:, None] == col_y[None]) * tap_of(from_z[:, None] - col_z[None])
    row = np.arange(2 * YZ)
    row_y = np.where(row < YZ, row // BZ, np.where(row < YZ * 3 // 2, (row - YZ) // BZ - RADIUS, (row - YZ) // BZ - RADIUS + BY))
    full_y = ((row % BZ)[:, None] == col_z[None]) * tap_of(row_y[:, None] - col_y[None])
    out = np.arange(ROWS)
    src = np.arange(3 * ROWS)
    full_x = ((src % CH)[None] == (out % CH)[:, None]) * tap_of((src // CH - BX)[None] - (out // CH)[:, None])
    return [jnp.asarray(m, BF16) for m in (pack, own_z, edges_z, full_y, full_x)]


def kernel(
    nx, ny, nz,
    live_ref, w_hbm, x_hbm, pack_hbm, ownz_hbm, edgez_hbm, fully_hbm, fullx_hbm,
    out_ref, tc_ref,
    wraw, src, wmap, xdat, pack, ownz, edgez, fully, fullx,
    zpack, fz, fyz, smooth, ze, ye, xe, grad, mixw, mixg, graw,
    cpart, rp, rx, c1, c2, etot, ep, ex,
    load_sem, hs, hr, ps, pr, xs, xr, gs, gr, eps, epr, exs, exr,
):
    ix, iy, iz = lax.axis_index("gx"), lax.axis_index("gy"), lax.axis_index("gz")
    lanes_y = T // ny
    rows_z = PR // nz
    plane = nz * ny
    cells = float(K * BX * BY * BZ * nx * ny * nz)

    loads = [
        pltpu.make_async_copy(a, b, load_sem.at[i])
        for i, (a, b) in enumerate(
            [(w_hbm, wraw), (pack_hbm, pack), (ownz_hbm, ownz), (edgez_hbm, edgez), (fully_hbm, fully),
             (fullx_hbm, fullx), (x_hbm, xdat)]
        )
    ]
    for load in loads:
        load.start()

    def plane_peers():
        for d in range(1, plane):
            yield d, lax.rem(iz + d // ny, nz), lax.rem(iy + d % ny, ny)

    def line_peers():
        for d in range(1, nx):
            yield d, lax.rem(ix + d, nx)

    barrier = pltpu.get_barrier_semaphore()
    for d, pz, py in plane_peers():
        pl.semaphore_signal(barrier, inc=1, device_id={"gz": pz, "gy": py}, device_id_type=MESH)
    for d, px in line_peers():
        pl.semaphore_signal(barrier, inc=1, device_id={"gx": px}, device_id_type=MESH)

    @pl.when(ix == 0)
    def _():
        xe[:, 0] = jnp.zeros_like(xe[:, 0])

    @pl.when(ix == nx - 1)
    def _():
        xe[:, 1] = jnp.zeros_like(xe[:, 1])

    @pl.when(iy == 0)
    def _():
        ye[:, :, :, : YZ // 2] = jnp.zeros_like(ye[:, :, :, : YZ // 2])

    @pl.when(iy == ny - 1)
    def _():
        ye[:, :, :, YZ // 2 :] = jnp.zeros_like(ye[:, :, :, YZ // 2 :])

    @pl.when(iz == 0)
    def _():
        ze[:, :, :, :128] = jnp.zeros_like(ze[:, :, :, :128])

    @pl.when(iz == nz - 1)
    def _():
        ze[:, :, :, 128:] = jnp.zeros_like(ze[:, :, :, 128:])

    loads[0].wait()
    for x in range(BX):
        wmap[x] = jnp.transpose(wraw[pl.ds(x * YZ, YZ), :])
        src[x] = wmap[x].astype(BF16)

    def dot(a, b):
        return jnp.dot(a, b, preferred_element_type=F32)

    def exact(a, b):
        return jnp.dot(a, b, precision=HIGH, preferred_element_type=F32)

    def remote(a, b, ssem, rsem, to):
        return pltpu.make_async_remote_copy(
            src_ref=a, dst_ref=b, send_sem=ssem, recv_sem=rsem, device_id=to, device_id_type=MESH
        )

    def maps(g):
        return pl.ds(g * CH, CH)

    def halo(s, g, axis):
        k, half = maps(g), YZ // 2
        if axis == "z":
            down = (0, zpack.at[:, k, pl.ds(0, 128)], ze.at[s, :, k, pl.ds(128, 128)])
            up = (1, zpack.at[:, k, pl.ds(128, 128)], ze.at[s, :, k, pl.ds(0, 128)])
            me, n = iz, nz
        elif axis == "y":
            down = (2, fz.at[:, k, pl.ds(0, half)], ye.at[s, :, k, pl.ds(half, half)])
            up = (3, fz.at[:, k, pl.ds(half, half)], ye.at[s, :, k, pl.ds(0, half)])
            me, n = iy, ny
        else:
            down = (4, fyz.at[:, k, :], xe.at[s, 1, :, k, :])
            up = (5, fyz.at[:, k, :], xe.at[s, 0, :, k, :])
            me, n = ix, nx

        def copy(i, a, b, to):
            return remote(a, b, hs.at[s, g, i], hr.at[s, g, i], {"g" + axis: to})

        return (
            (me > 0, me < n - 1, copy(*down, lax.rem(me + n - 1, n))),
            (me < n - 1, me > 0, copy(*up, lax.rem(me + 1, n))),
        )

    def send(s, g, axis):
        for sends, _, copy in halo(s, g, axis):
            @pl.when(sends)
            def _():
                copy.start()

    def receive(s, g, axis):
        for _, comes, copy in halo(s, g, axis):
            @pl.when(comes)
            def _():
                copy.wait_recv()

    def sent(s, g, axis):
        if s < 0:
            return
        for sends, _, copy in halo(s, g, axis):
            @pl.when(sends)
            def _():
                copy.wait_send()

    count = live_ref[0, 0, 0]
    row_y = lax.broadcasted_iota(jnp.int32, (1, YZ), 1) // BZ

    def mask_of(x):
        return x * BY + row_y < count

    def pack_z(s, g):
        k = maps(g)
        sent(s - 1, g, "z")
        zpack[:, k, :] = dot(src[:, k, :].reshape(ROWS, YZ), pack[...]).astype(BF16).reshape(BX, CH, 2 * 128)

    def send_z(s, g):
        send(s, g, "z")

    def filter_z(s, g):
        k = maps(g)
        sent(s - 1, g, "y")
        field = src[:, k, :].reshape(ROWS, YZ)
        own = jnp.concatenate([dot(field[:, : YZ // 2], ownz[...]), dot(field[:, YZ // 2 :], ownz[...])], axis=1)
        receive(s, g, "z")
        edges = dot(ze[s, :, k, :].reshape(ROWS, 2 * 128), edgez[...])
        fz[:, k, :] = (own + edges).astype(BF16).reshape(BX, CH, YZ)
        send(s, g, "y")

    def filter_y(s, g):
        k = maps(g)
        sent(s - 1, g, "x")
        receive(s, g, "y")
        field = jnp.concatenate([fz[:, k, :].reshape(ROWS, YZ), ye[s, :, k, :].reshape(ROWS, YZ)], axis=1)
        fyz[:, k, :] = dot(field, fully[...]).astype(BF16).reshape(BX, CH, YZ)
        send(s, g, "x")

    def filter_x(s, g):
        k = maps(g)
        receive(s, g, "x")
        field = jnp.concatenate(
            [xe[s, 0, :, k, :].reshape(ROWS, YZ), fyz[:, k, :].reshape(ROWS, YZ), xe[s, 1, :, k, :].reshape(ROWS, YZ)],
            axis=0,
        )
        return dot(fullx[...], field).reshape(BX, CH, YZ)

    def groups(p):
        return range(p * PAIR, (p + 1) * PAIR)

    def contribution(s, p):
        for g in groups(p):
            value = filter_x(s, g)
            for x in range(BX):
                smooth[x, maps(g), :] = jnp.where(mask_of(x), value[x], 0.0).astype(BF16)
        k = pl.ds(p * PR, PR)
        total = dot(smooth[0, k, :], xdat[pl.ds(0, YZ), :])
        for x in range(1, BX):
            total += dot(smooth[x, k, :], xdat[pl.ds(x * YZ, YZ), :])
        return total

    def gradient(p, courses):
        for x in range(BX):
            value = lax.dot_general(
                courses, xdat[pl.ds(x * YZ, YZ), :], (((1,), (1,)), ((), ())), preferred_element_type=F32
            )
            src[x, pl.ds(p * PR, PR), :] = jnp.where(mask_of(x), value, 0.0).astype(BF16)

    def square_sum(value):
        total = value[0] * value[0]
        for x in range(1, BX):
            total += value[x] * value[x]
        return jnp.sum(total)

    def piece(j_z, j_y):
        return pl.ds(pl.multiple_of(j_z * rows_z, rows_z), rows_z), pl.ds(pl.multiple_of(j_y * lanes_y, lanes_y), lanes_y)

    def height(a):
        return rows_z + 8 * a

    def reduce_start(a, g, value, energy):
        i = 2 * a + g
        for j in range(nz):
            cpart[i, j, :rows_z] = value[j * rows_z : (j + 1) * rows_z]
            if a:
                cpart[i, j, rows_z:] = jnp.full((8, T), energy, F32)
        for d, pz, py in plane_peers():
            reduce_copy(a, g, d, pz, py, iz * ny + iy).start()

    def reduce_copy(a, g, d, pz, py, slot):
        i, h = 2 * a + g, pl.ds(0, height(a))
        lanes = pl.ds(pl.multiple_of(py * lanes_y, lanes_y), lanes_y)
        return remote(
            cpart.at[i, pz, h, lanes], rp.at[i, slot, h], ps.at[i, d - 1], pr.at[i, slot], {"gz": pz, "gy": py}
        )

    def line_copy(a, g, d, px, slot):
        i, h = 2 * a + g, pl.ds(0, height(a))
        return remote(rx.at[i, nx, h], rx.at[i, slot, h], xs.at[i, d - 1], xr.at[i, slot], {"gx": px})

    def gather_copy(a, g, d, pz, py, z, y):
        i = 2 * a + g
        rows, lanes = piece(z, y)
        there = (c1, c2)[a].at[g, rows, lanes]
        return remote(there, there, gs.at[i, d - 1], gr.at[i, z * ny + y], {"gz": pz, "gy": py})

    def tree(parts):
        while len(parts) > 1:
            parts = [p + q for p, q in zip(parts[::2], parts[1::2])] + ([parts[-1]] if len(parts) % 2 else [])
        return parts[0]

    def reduce_line(a, g):
        i, h = 2 * a + g, height(a)
        for d, pz, py in plane_peers():
            reduce_copy(a, g, d, pz, py, pz * ny + py).wait_recv()
        lanes = pl.ds(pl.multiple_of(iy * lanes_y, lanes_y), lanes_y)
        rp[i, iz * ny + iy, :h] = cpart[i, iz, :h, lanes]
        rx[i, nx, :h] = tree([rp[i, j, :h] for j in range(plane)])
        for d, px in line_peers():
            line_copy(a, g, d, px, ix).start()

    def reduce_gather(a, g):
        i, h = 2 * a + g, height(a)
        for d, px in line_peers():
            line_copy(a, g, d, px, px).wait_recv()
        rx[i, ix, :h] = rx[i, nx, :h]
        total = tree([rx[i, j, :h] for j in range(nx)])
        rows, lanes = piece(iz, iy)
        (c1, c2)[a][g, rows, lanes] = total[:rows_z]
        if a:
            etot[g] = total[rows_z:]
        for d, pz, py in plane_peers():
            gather_copy(a, g, d, pz, py, iz, iy).start()

    def reduce_end(a, g):
        for d, pz, py in plane_peers():
            gather_copy(a, g, d, pz, py, pz, py).wait_recv()

    def gram_of(courses):
        gram = lax.dot_general(courses, courses, (((1,), (1,)), ((), ())), precision=HIGH, preferred_element_type=F32)
        diag = lax.broadcasted_iota(jnp.int32, (K, K), 0) == lax.broadcasted_iota(jnp.int32, (K, K), 1)
        return float(K) / jnp.sum(jnp.where(diag, gram, 0.0)) * gram

    known = {}

    def reduce_first(p):
        reduce_start(0, p, contribution(0, p), None)

    def first_gradient(p):
        reduce_end(0, p)
        gradient(p, c1[p].astype(BF16))
        for g in groups(p):
            pack_z(1, g)
            send_z(1, g)

    def second_source(g):
        value = filter_x(1, g)
        grad[:, maps(g), :] = value
        src[:, maps(g), :] = value.astype(BF16)
        pack_z(2, g)
        send_z(2, g)
        known["energy", g] = square_sum(value)

    def reduce_second(p):
        reduce_start(1, p, contribution(2, p), sum(known["energy", g] for g in groups(p)))

    def second_gradient(p):
        reduce_end(1, p)
        gradient(p, c2[p].astype(BF16))
        for g in groups(p):
            pack_z(3, g)
            send_z(3, g)

    def mix_maps():
        known["decay1"] = gram_of(c1[...].reshape(K, T))
        for x in range(BX):
            mixw[x] = wmap[x] - 0.5 * exact(known["decay1"], wmap[x])

    def mix_gradient():
        for x in range(BX):
            mixg[x] = grad[x] - 0.5 * exact(known["decay1"], grad[x])

    def second_courses():
        first = c1[...].reshape(K, T)
        scale = 1.0 / jnp.sqrt((etot[0, 0:1, 0:1] + etot[1, 0:1, 0:1]) / cells + 1e-06)
        known["scale1"] = scale
        courses = first + 0.5 * (scale * c2[...].reshape(K, T) - exact(known["decay1"], first))
        tc_ref[...] = courses.astype(BF16)
        decay = gram_of(courses)
        for x in range(BX):
            now = mixw[x] + 0.5 * scale * grad[x]
            out_ref[pl.ds(x * YZ, YZ), :] = jnp.transpose(now - 0.5 * exact(decay, now))

    def second_result(g):
        value = mixg[:, maps(g), :] + 0.5 * known["scale1"] * filter_x(3, g)
        mixg[:, maps(g), :] = value
        known["energy", g] = square_sum(value)

    every, pairs = range(NC), range(NP)
    loads[1].wait()
    for g in every:
        pack_z(0, g)
    pl.semaphore_wait(barrier, plane - 1 + nx - 1)
    for g in every:
        send_z(0, g)
    loads[2].wait()
    loads[3].wait()
    for g in every:
        filter_z(0, g)
    loads[4].wait()
    for g in every:
        filter_y(0, g)
    loads[5].wait()
    loads[6].wait()
    for step in (reduce_first, lambda p: reduce_line(0, p), lambda p: reduce_gather(0, p), first_gradient):
        for p in pairs:
            step(p)
    for g in every:
        filter_z(1, g)
    for g in every:
        filter_y(1, g)
    mix_maps()
    second_source(0)
    second_source(1)
    filter_z(2, 0)
    second_source(2)
    filter_z(2, 1)
    second_source(3)
    filter_y(2, 0)
    filter_z(2, 2)
    filter_y(2, 1)
    filter_z(2, 3)
    filter_y(2, 2)
    filter_y(2, 3)
    mix_gradient()
    for step in (reduce_second, lambda p: reduce_line(1, p), lambda p: reduce_gather(1, p), second_gradient):
        for p in pairs:
            step(p)
    for g in every:
        filter_z(3, g)
    for g in every:
        filter_y(3, g)
    second_courses()
    for g in every:
        second_result(g)
    me = iz * ny + iy
    ep[plane] = jnp.full((8, 128), sum(known["energy", g] for g in every), F32)

    def energy_plane(d, pz, py, slot):
        return remote(ep.at[plane], ep.at[slot], eps.at[d - 1], epr.at[slot], {"gz": pz, "gy": py})

    def energy_line(d, px, slot):
        return remote(ex.at[nx], ex.at[slot], exs.at[d - 1], exr.at[slot], {"gx": px})

    for d, pz, py in plane_peers():
        energy_plane(d, pz, py, me).start()
    for x in range(BX):
        graw[pl.ds(x * YZ, YZ), :] = jnp.transpose(mixg[x])
    for d, pz, py in plane_peers():
        energy_plane(d, pz, py, pz * ny + py).wait_recv()
    ep[me] = ep[plane]
    ex[nx] = tree([ep[j] for j in range(plane)])
    for d, px in line_peers():
        energy_line(d, px, ix).start()
    for g in every:
        for axis in "zyx":
            sent(3, g, axis)
    for a in (0, 1):
        for g in pairs:
            for d, pz, py in plane_peers():
                reduce_copy(a, g, d, pz, py, me).wait_send()
                gather_copy(a, g, d, pz, py, iz, iy).wait_send()
            for d, px in line_peers():
                line_copy(a, g, d, px, ix).wait_send()
    for d, pz, py in plane_peers():
        energy_plane(d, pz, py, me).wait_send()
    for d, px in line_peers():
        energy_line(d, px, px).wait_recv()
    ex[ix] = ex[nx]
    total = tree([ex[j] for j in range(nx)])
    half_scale = 0.5 / jnp.sqrt(total[0:1, 0:1] / cells + 1e-06)
    for x in range(BX):
        rows = pl.ds(x * YZ, YZ)
        out_ref[rows, :] = out_ref[rows, :] + half_scale * graw[rows, :]
    for d, px in line_peers():
        energy_line(d, px, ix).wait_send()


def per_device(nx, ny, nz, bold_data, spatial_maps, live_blocks):
    rows_z, lanes_y, plane = PR // nz, T // ny, ny * nz
    voxels = jnp.transpose(spatial_maps, (1, 2, 3, 0)).reshape(BX * YZ, K)
    matrices = filter_matrices()
    vmem, dma = pltpu.VMEM, pltpu.SemaphoreType.DMA
    field, wide, raw = vmem((BX, K, YZ), BF16), vmem((BX, K, YZ), F32), vmem((BX * YZ, K), F32)
    new_maps, courses = pl.pallas_call(
        functools.partial(kernel, nx, ny, nz),
        out_shape=(jax.ShapeDtypeStruct((BX * YZ, K), F32), jax.ShapeDtypeStruct((K, T), BF16)),
        in_specs=[pl.BlockSpec(memory_space=pltpu.SMEM)] + [pl.BlockSpec(memory_space=pl.ANY)] * 7,
        out_specs=(pl.BlockSpec(memory_space=pltpu.VMEM), pl.BlockSpec(memory_space=pltpu.VMEM)),
        scratch_shapes=[
            raw, field, wide, vmem((BX * YZ, T), BF16),
            *[vmem(m.shape, BF16) for m in matrices],
            vmem((BX, K, 256), BF16), field, field, field,
            vmem((4, BX, K, 256), BF16), vmem((4, BX, K, YZ), BF16), vmem((4, 2, BX, K, YZ), BF16),
            wide, wide, wide, raw,
            vmem((4, nz, rows_z + 8, T), F32), vmem((4, plane, rows_z + 8, lanes_y), F32),
            vmem((4, nx + 1, rows_z + 8, lanes_y), F32),
            vmem((NP, PR, T), F32), vmem((NP, PR, T), F32), vmem((NP, 8, lanes_y), F32),
            vmem((plane + 1, 8, 128), F32), vmem((nx + 1, 8, 128), F32),
            dma((7,)), dma((4, NC, 6)), dma((4, NC, 6)),
            dma((4, plane)), dma((4, plane)), dma((4, nx)), dma((4, nx)), dma((4, plane)), dma((4, plane)),
            dma((plane,)), dma((plane,)), dma((nx,)), dma((nx,)),
        ],
        compiler_params=pltpu.CompilerParams(
            collective_id=0, has_side_effects=True, vmem_limit_bytes=56 * 1024 * 1024
        ),
    )(live_blocks, voxels, bold_data.reshape(BX * YZ, T), *matrices)
    new_maps = jnp.transpose(new_maps.reshape(BX, BY, BZ, K), (3, 0, 1, 2))
    return new_maps, courses


def solution(mesh):
    return jax.shard_map(
        functools.partial(per_device, mesh.shape["gx"], mesh.shape["gy"], mesh.shape["gz"]),
        mesh=mesh,
        in_specs=(P("gx", "gy", "gz", None), P(None, "gx", "gy", "gz"), P("gx", "gy", "gz")),
        out_specs=(P(None, "gx", "gy", "gz"), P()),
        check_vma=False,
    )
```

time: 1310 us -> 140 us (0.11)
  waiting for transfers between devices: 512 us -> 0 us
  local copies, waits for them, and re-layouts: 341 us -> 3.75 us
  matrix products: 153 us -> 0 us
  Pallas kernels: 0 us -> 135 us
  blocking collectives: 135 us -> 0 us
  starting transfers between devices: 79.6 us -> 0 us
  other arithmetic: 61 us -> 0 us
  between operations: 18.1 us -> 1.29 us
    psum x2 -> x0, waiting for transfers between devices: 290 us -> none  [per_device(): courses = lax.psum(partial_courses, ('gx', 'gy', 'gz'))]
    ppermute x24 -> x0, waiting for transfers between devices: 222 us -> none  [the longest x12 169 us: extended(): after = lax.ppermute(leading, axis, down)]
    dot_general x20 -> x0, matrix products: 153 us -> none  [the longest x12 135 us: filter_along(): jnp.tensordot(field, band, axes=((axis,), (0,)), precision=lax.Precision....]
    slice x19 -> x0, local copies, waits for them, and re-layouts: 152 us -> none  [the longest x13 98.7 us: extended(): last = lax.slice_in_dim(x, length - width, length, axis=dim)]
    psum x2 -> x0, blocking collectives: 135 us -> none  [per_device(): energy = lax.psum(jnp.sum(grad * grad), ('gx', 'gy', 'gz')) / all_cells]
    pallas_call x0 -> x1, Pallas kernels: none -> 135 us  [per_device(): pl.pallas_call(functools.partial(kernel, nx, ny, nz), out_shape=(jax.Shap...]
    ppermute x18 -> x0, local copies, waits for them, and re-layouts: 134 us -> none  [the longest x9 67.1 us: extended(): before = lax.ppermute(last, axis, up)]
    ppermute x24 -> x0, starting transfers between devices: 79.5 us -> none  [the longest x12 61.5 us: extended(): before = lax.ppermute(last, axis, up)]
  transfers between devices with their start and end apart: 26 -> 0, of which waited for: 22 -> 0; matrix products, arithmetic and copies ran while one was open for 10% -> 0% of each run, Pallas kernels for 0% -> 0%
where the time goes in v2:
time: 140 us
  Pallas kernels  135 us (96%)
  local copies, waits for them, and re-layouts  3.75 us (3%)
    pallas_call x1, Pallas kernels, per_device(): pl.pallas_call(functools.partial(kernel, nx, ny, nz), out_shape=(jax.Shap...  135 us
    unnamed x4, local copies, waits for them, and re-layouts  3.75 us

profile of v2, /device:TPU:1, one launch (start us, length us, event | category | flops | bytes accessed | tf_op | source)
XLA Modules:
  0.0 139.9 jit_solution(12777198217987545449)
XLA Ops:
  1.3 134.8 %shard_map.95 = (f32[4096,64]{1,0:T(8,128)}, bf16[64,512]{1,0:T(8,128)(2,1)}) custom-call(s32[1,1,1]{2,1,0:T(1,128)S(6)} %copy.12.live_ref, f32[4096,64]{1,0:T(8,128)} %bitcast.9, bf16[4096,512]{1,0:T(8,128)(2,1)} %bitcast.7, bf16[512,256]{1,0:T(8,128)(2,1)} %constant.10.clone.pack_hbm, bf16[256,256]{1,0:T(8,128)(2,1)} %constant.11.clone.ownz_hbm, ...), custom_call_target="tpu_custom_call" | custom-call | tf_op jit(solution)/shard_map/pallas_call | solution.py:466
  136.1 0.0 copy-start
  136.1 3.1 %copy.13 = f32[64,8,16,32]{0,3,2,1:T(8,128)} copy(f32[64,8,16,32]{0,3,2,1:T(8,128)} %bitcast.8) | data formatting | bytes 2097152
  139.2 0.0 copy-done
  139.3 0.6 copy.14
Async XLA Ops:
  136.1 3.1 %copy-start = (bf16[64,512]{1,0:T(8,128)(2,1)S(1)}, bf16[64,512]{1,0:T(8,128)(2,1)}, u32[]{:S(2)}) copy-start(bf16[64,512]{1,0:T(8,128)(2,1)} %get-tuple-element.9) | copy-start | bytes 196612

commit v3 on v2

--- a/solution.py
+++ b/solution.py
@@ -37,25 +37,26 @@
     low = edge < BY * RADIUS
     edge_z = np.where(low, edge % RADIUS, BZ - RADIUS + edge % RADIUS)
     pack = (col_y[:, None] == edge_y[None]) & (col_z[:, None] == edge_z[None])
-    half_y, half_z = col_y[: YZ // 2], col_z[: YZ // 2]
-    own_z = (half_y[:, None] == half_y[None]) * tap_of(half_z[:, None] - half_z[None])
-    from_z = np.where(low, edge % RADIUS - RADIUS, BZ + edge % RADIUS)
-    edges_z = (edge_y[:, None] == col_y[None]) * tap_of(from_z[:, None] - col_z[None])
-    row = np.arange(2 * YZ)
-    row_y = np.where(row < YZ, row // BZ, np.where(row < YZ * 3 // 2, (row - YZ) // BZ - RADIUS, (row - YZ) // BZ - RADIUS + BY))
-    full_y = ((row % BZ)[:, None] == col_z[None]) * tap_of(row_y[:, None] - col_y[None])
+    near = np.arange(BY * RADIUS) // RADIUS
+    corner = np.arange(4 * RADIUS * RADIUS)
+    corner_y = (corner % RADIUS**2) // RADIUS + np.where(corner // RADIUS**2 % 2 == 0, -RADIUS, BY)
+    corner_z = corner % RADIUS + np.where(corner < 2 * RADIUS**2, -RADIUS, BZ)
+    half = col[: YZ // 2]
+    row_y = np.concatenate([col_y, half // BZ - RADIUS, half // BZ + BY, near, near, corner_y])
+    row_z = np.concatenate([col_z, half % BZ, half % BZ, edge % RADIUS + np.where(low, -RADIUS, BZ), corner_z])
+    full_yz = tap_of(row_y[:, None] - col_y[None]) * tap_of(row_z[:, None] - col_z[None])
     out = np.arange(ROWS)
     src = np.arange(3 * ROWS)
     full_x = ((src % CH)[None] == (out % CH)[:, None]) * tap_of((src // CH - BX)[None] - (out // CH)[:, None])
-    return [jnp.asarray(m, BF16) for m in (pack, own_z, edges_z, full_y, full_x)]
+    return [jnp.asarray(m, BF16) for m in (pack, full_yz, full_x)]
 
 
 def kernel(
     nx, ny, nz,
-    live_ref, w_hbm, x_hbm, pack_hbm, ownz_hbm, edgez_hbm, fully_hbm, fullx_hbm,
+    live_ref, w_hbm, x_hbm, pack_hbm, full_hbm, fullx_hbm,
     out_ref, tc_ref,
-    wraw, src, wmap, xdat, pack, ownz, edgez, fully, fullx,
-    zpack, fz, fyz, smooth, ze, ye, xe, grad, mixw, mixg, graw,
+    wraw, src, wmap, xdat, pack, full, fullx,
+    zpack, cpack, fyz, smooth, ze, ye, ce, xe, grad, mixw, mixg, graw,
     cpart, rp, rx, c1, c2, etot, ep, ex,
     load_sem, hs, hr, ps, pr, xs, xr, gs, gr, eps, epr, exs, exr,
 ):
@@ -67,13 +68,10 @@
 
     loads = [
         pltpu.make_async_copy(a, b, load_sem.at[i])
-        for i, (a, b) in enumerate(
-            [(w_hbm, wraw), (pack_hbm, pack), (ownz_hbm, ownz), (edgez_hbm, edgez), (fully_hbm, fully),
-             (fullx_hbm, fullx), (x_hbm, xdat)]
-        )
+        for i, (a, b) in enumerate([(w_hbm, wraw), (pack_hbm, pack), (full_hbm, full), (fullx_hbm, fullx), (x_hbm, xdat)])
     ]
-    for load in loads:
-        load.start()
+    loads[0].start()
+    loads[1].start()
 
     def plane_peers():
         for d in range(1, plane):
@@ -113,10 +111,20 @@
     def _():
         ze[:, :, :, 128:] = jnp.zeros_like(ze[:, :, :, 128:])
 
+    for i, (gone_y, gone_z) in enumerate(((0, 0), (ny - 1, 0), (0, nz - 1), (ny - 1, nz - 1))):
+        @pl.when((iy == gone_y) | (iz == gone_z))
+        def _():
+            ce[:, i] = jnp.zeros_like(ce[:, i])
+
     loads[0].wait()
-    for x in range(BX):
-        wmap[x] = jnp.transpose(wraw[pl.ds(x * YZ, YZ), :])
+    for load in loads[2:]:
+        load.start()
+
+    @pl.loop(0, BX)
+    def _(x):
+        wmap[x] = jnp.transpose(wraw[pl.ds(pl.multiple_of(x * YZ, YZ), YZ), :])
         src[x] = wmap[x].astype(BF16)
+
 
     def dot(a, b):
         return jnp.dot(a, b, preferred_element_type=F32)
@@ -134,25 +142,36 @@
 
     def halo(s, g, axis):
         k, half = maps(g), YZ // 2
+        up_y, down_y = lax.rem(iy + 1, ny), lax.rem(iy + ny - 1, ny)
+        up_z, down_z = lax.rem(iz + 1, nz), lax.rem(iz + nz - 1, nz)
+        low_y, high_y, low_z, high_z = iy > 0, iy < ny - 1, iz > 0, iz < nz - 1
+
+        def copy(i, a, b, to):
+            return remote(a, b, hs.at[s, g, i], hr.at[s, g, i], to)
+
         if axis == "z":
-            down = (0, zpack.at[:, k, pl.ds(0, 128)], ze.at[s, :, k, pl.ds(128, 128)])
-            up = (1, zpack.at[:, k, pl.ds(128, 128)], ze.at[s, :, k, pl.ds(0, 128)])
-            me, n = iz, nz
-        elif axis == "y":
-            down = (2, fz.at[:, k, pl.ds(0, half)], ye.at[s, :, k, pl.ds(half, half)])
-            up = (3, fz.at[:, k, pl.ds(half, half)], ye.at[s, :, k, pl.ds(0, half)])
-            me, n = iy, ny
-        else:
-            down = (4, fyz.at[:, k, :], xe.at[s, 1, :, k, :])
-            up = (5, fyz.at[:, k, :], xe.at[s, 0, :, k, :])
-            me, n = ix, nx
-
-        def copy(i, a, b, to):
-            return remote(a, b, hs.at[s, g, i], hr.at[s, g, i], {"g" + axis: to})
-
+            return (
+                (low_z, high_z, copy(0, zpack.at[:, k, pl.ds(0, 128)], ze.at[s, :, k, pl.ds(128, 128)], {"gz": down_z})),
+                (high_z, low_z, copy(1, zpack.at[:, k, pl.ds(128, 128)], ze.at[s, :, k, pl.ds(0, 128)], {"gz": up_z})),
+            )
+        if axis == "y":
+            return (
+                (low_y, high_y, copy(2, src.at[:, k, pl.ds(0, half)], ye.at[s, :, k, pl.ds(half, half)], {"gy": down_y})),
+                (high_y, low_y, copy(3, src.at[:, k, pl.ds(half, half)], ye.at[s, :, k, pl.ds(0, half)], {"gy": up_y})),
+            )
+        if axis == "c":
+            ways = (
+                (high_y & high_z, low_y & low_z, up_y, up_z), (low_y & high_z, high_y & low_z, down_y, up_z),
+                (high_y & low_z, low_y & high_z, up_y, down_z), (low_y & low_z, high_y & high_z, down_y, down_z),
+            )
+            return tuple(
+                (sends, comes, copy(6 + i, cpack.at[i, :, k, :], ce.at[s, i, :, k, :], {"gy": to_y, "gz": to_z}))
+                for i, (sends, comes, to_y, to_z) in enumerate(ways)
+            )
+        down_x, up_x = lax.rem(ix + nx - 1, nx), lax.rem(ix + 1, nx)
         return (
-            (me > 0, me < n - 1, copy(*down, lax.rem(me + n - 1, n))),
-            (me < n - 1, me > 0, copy(*up, lax.rem(me + 1, n))),
+            (ix > 0, ix < nx - 1, copy(4, fyz.at[:, k, :], xe.at[s, 1, :, k, :], {"gx": down_x})),
+            (ix < nx - 1, ix > 0, copy(5, fyz.at[:, k, :], xe.at[s, 0, :, k, :], {"gx": up_x})),
         )
 
     def send(s, g, axis):
@@ -181,30 +200,40 @@
     def mask_of(x):
         return x * BY + row_y < count
 
+    first_half = lax.broadcasted_iota(jnp.int32, (ROWS // 2, 128), 1) < 64
+
+    def joined(a, b):
+        return jnp.where(first_half, a, pltpu.roll(b, 64, 1)), jnp.where(first_half, pltpu.roll(a, 64, 1), b)
+
     def pack_z(s, g):
         k = maps(g)
         sent(s - 1, g, "z")
-        zpack[:, k, :] = dot(src[:, k, :].reshape(ROWS, YZ), pack[...]).astype(BF16).reshape(BX, CH, 2 * 128)
+        sent(s - 1, g, "c")
+        edges = dot(src[:, k, :].reshape(ROWS, YZ), pack[...])
+        zpack[:, k, :] = edges.astype(BF16).reshape(BX, CH, 2 * 128)
+        for i, lanes in ((2, slice(0, 128)), (0, slice(128, 256))):
+            low, high = joined(edges[: ROWS // 2, lanes], edges[ROWS // 2 :, lanes])
+            cpack[i, :, k, :] = high.astype(BF16).reshape(BX // 2, CH, 128)
+            cpack[i + 1, :, k, :] = low.astype(BF16).reshape(BX // 2, CH, 128)
 
     def send_z(s, g):
+        send(s, g, "y")
+        send(s, g, "c")
         send(s, g, "z")
 
-    def filter_z(s, g):
-        k = maps(g)
-        sent(s - 1, g, "y")
-        field = src[:, k, :].reshape(ROWS, YZ)
-        own = jnp.concatenate([dot(field[:, : YZ // 2], ownz[...]), dot(field[:, YZ // 2 :], ownz[...])], axis=1)
-        receive(s, g, "z")
-        edges = dot(ze[s, :, k, :].reshape(ROWS, 2 * 128), edgez[...])
-        fz[:, k, :] = (own + edges).astype(BF16).reshape(BX, CH, YZ)
-        send(s, g, "y")
-
-    def filter_y(s, g):
+    def filter_yz(s, g):
         k = maps(g)
         sent(s - 1, g, "x")
-        receive(s, g, "y")
-        field = jnp.concatenate([fz[:, k, :].reshape(ROWS, YZ), ye[s, :, k, :].reshape(ROWS, YZ)], axis=1)
-        fyz[:, k, :] = dot(field, fully[...]).astype(BF16).reshape(BX, CH, YZ)
+        own = dot(src[:, k, :].reshape(ROWS, YZ), full[pl.ds(0, YZ), :])
+        for axis in "zyc":
+            receive(s, g, axis)
+        corners = [ce[s, i, :, k, :].reshape(ROWS // 2, 128).astype(F32) for i in range(4)]
+        low, high = joined(*corners[:2]), joined(*corners[2:])
+        corners = jnp.concatenate(
+            [jnp.concatenate([low[0], high[0]], axis=1), jnp.concatenate([low[1], high[1]], axis=1)], axis=0
+        ).astype(BF16)
+        field = jnp.concatenate([ye[s, :, k, :].reshape(ROWS, YZ), ze[s, :, k, :].reshape(ROWS, 2 * 128), corners], axis=1)
+        fyz[:, k, :] = (own + dot(field, full[pl.ds(YZ, 2 * YZ), :])).astype(BF16).reshape(BX, CH, YZ)
         send(s, g, "x")
 
     def filter_x(s, g):
@@ -230,7 +259,9 @@
             total += dot(smooth[x, k, :], xdat[pl.ds(x * YZ, YZ), :])
         return total
 
-    def gradient(p, courses):
+    def gradient(s, p, courses):
+        for g in groups(p):
+            sent(s - 1, g, "y")
         for x in range(BX):
             value = lax.dot_general(
                 courses, xdat[pl.ds(x * YZ, YZ), :], (((1,), (1,)), ((), ())), preferred_element_type=F32
@@ -319,13 +350,14 @@
 
     def first_gradient(p):
         reduce_end(0, p)
-        gradient(p, c1[p].astype(BF16))
+        gradient(1, p, c1[p].astype(BF16))
         for g in groups(p):
             pack_z(1, g)
             send_z(1, g)
 
     def second_source(g):
         value = filter_x(1, g)
+        sent(1, g, "y")
         grad[:, maps(g), :] = value
         src[:, maps(g), :] = value.astype(BF16)
         pack_z(2, g)
@@ -337,18 +369,20 @@
 
     def second_gradient(p):
         reduce_end(1, p)
-        gradient(p, c2[p].astype(BF16))
+        gradient(3, p, c2[p].astype(BF16))
         for g in groups(p):
             pack_z(3, g)
             send_z(3, g)
 
     def mix_maps():
         known["decay1"] = gram_of(c1[...].reshape(K, T))
-        for x in range(BX):
+        @pl.loop(0, BX)
+        def _(x):
             mixw[x] = wmap[x] - 0.5 * exact(known["decay1"], wmap[x])
 
     def mix_gradient():
-        for x in range(BX):
+        @pl.loop(0, BX)
+        def _(x):
             mixg[x] = grad[x] - 0.5 * exact(known["decay1"], grad[x])
 
     def second_courses():
@@ -358,9 +392,11 @@
         courses = first + 0.5 * (scale * c2[...].reshape(K, T) - exact(known["decay1"], first))
         tc_ref[...] = courses.astype(BF16)
         decay = gram_of(courses)
-        for x in range(BX):
+
+        @pl.loop(0, BX)
+        def _(x):
             now = mixw[x] + 0.5 * scale * grad[x]
-            out_ref[pl.ds(x * YZ, YZ), :] = jnp.transpose(now - 0.5 * exact(decay, now))
+            out_ref[pl.ds(pl.multiple_of(x * YZ, YZ), YZ), :] = jnp.transpose(now - 0.5 * exact(decay, now))
 
     def second_result(g):
         value = mixg[:, maps(g), :] + 0.5 * known["scale1"] * filter_x(3, g)
@@ -375,42 +411,30 @@
     for g in every:
         send_z(0, g)
     loads[2].wait()
+    for g in every:
+        filter_yz(0, g)
     loads[3].wait()
-    for g in every:
-        filter_z(0, g)
     loads[4].wait()
-    for g in every:
-        filter_y(0, g)
-    loads[5].wait()
-    loads[6].wait()
     for step in (reduce_first, lambda p: reduce_line(0, p), lambda p: reduce_gather(0, p), first_gradient):
         for p in pairs:
             step(p)
     for g in every:
-        filter_z(1, g)
-    for g in every:
-        filter_y(1, g)
+        filter_yz(1, g)
     mix_maps()
     second_source(0)
     second_source(1)
-    filter_z(2, 0)
+    filter_yz(2, 0)
     second_source(2)
-    filter_z(2, 1)
+    filter_yz(2, 1)
     second_source(3)
-    filter_y(2, 0)
-    filter_z(2, 2)
-    filter_y(2, 1)
-    filter_z(2, 3)
-    filter_y(2, 2)
-    filter_y(2, 3)
+    filter_yz(2, 2)
+    filter_yz(2, 3)
     mix_gradient()
     for step in (reduce_second, lambda p: reduce_line(1, p), lambda p: reduce_gather(1, p), second_gradient):
         for p in pairs:
             step(p)
     for g in every:
-        filter_z(3, g)
-    for g in every:
-        filter_y(3, g)
+        filter_yz(3, g)
     second_courses()
     for g in every:
         second_result(g)
@@ -425,8 +449,11 @@
 
     for d, pz, py in plane_peers():
         energy_plane(d, pz, py, me).start()
-    for x in range(BX):
-        graw[pl.ds(x * YZ, YZ), :] = jnp.transpose(mixg[x])
+
+    @pl.loop(0, BX)
+    def _(x):
+        graw[pl.ds(pl.multiple_of(x * YZ, YZ), YZ), :] = jnp.transpose(mixg[x])
+
     for d, pz, py in plane_peers():
         energy_plane(d, pz, py, pz * ny + py).wait_recv()
     ep[me] = ep[plane]
@@ -434,7 +461,7 @@
     for d, px in line_peers():
         energy_line(d, px, ix).start()
     for g in every:
-        for axis in "zyx":
+        for axis in "zycx":
             sent(3, g, axis)
     for a in (0, 1):
         for g in pairs:
@@ -466,19 +493,20 @@
     new_maps, courses = pl.pallas_call(
         functools.partial(kernel, nx, ny, nz),
         out_shape=(jax.ShapeDtypeStruct((BX * YZ, K), F32), jax.ShapeDtypeStruct((K, T), BF16)),
-        in_specs=[pl.BlockSpec(memory_space=pltpu.SMEM)] + [pl.BlockSpec(memory_space=pl.ANY)] * 7,
+        in_specs=[pl.BlockSpec(memory_space=pltpu.SMEM)] + [pl.BlockSpec(memory_space=pl.ANY)] * 5,
         out_specs=(pl.BlockSpec(memory_space=pltpu.VMEM), pl.BlockSpec(memory_space=pltpu.VMEM)),
         scratch_shapes=[
             raw, field, wide, vmem((BX * YZ, T), BF16),
             *[vmem(m.shape, BF16) for m in matrices],
-            vmem((BX, K, 256), BF16), field, field, field,
-            vmem((4, BX, K, 256), BF16), vmem((4, BX, K, YZ), BF16), vmem((4, 2, BX, K, YZ), BF16),
+            vmem((BX, K, 256), BF16), vmem((4, BX // 2, K, 128), BF16), field, field,
+            vmem((4, BX, K, 256), BF16), vmem((4, BX, K, YZ), BF16), vmem((4, 4, BX // 2, K, 128), BF16),
+            vmem((4, 2, BX, K, YZ), BF16),
             wide, wide, wide, raw,
             vmem((4, nz, rows_z + 8, T), F32), vmem((4, plane, rows_z + 8, lanes_y), F32),
             vmem((4, nx + 1, rows_z + 8, lanes_y), F32),
             vmem((NP, PR, T), F32), vmem((NP, PR, T), F32), vmem((NP, 8, lanes_y), F32),
             vmem((plane + 1, 8, 128), F32), vmem((nx + 1, 8, 128), F32),
-            dma((7,)), dma((4, NC, 6)), dma((4, NC, 6)),
+            dma((5,)), dma((4, NC, 10)), dma((4, NC, 10)),
             dma((4, plane)), dma((4, plane)), dma((4, nx)), dma((4, nx)), dma((4, plane)), dma((4, plane)),
             dma((plane,)), dma((plane,)), dma((nx,)), dma((nx,)),
         ],

time: 140 us -> 138 us (0.986)
  Pallas kernels: 135 us -> 132 us
    pallas_call x1, Pallas kernels: 135 us -> 132 us  [per_device(): pl.pallas_call(functools.partial(kernel, nx, ny, nz), out_shape=(jax.Shap...]
where the time goes in v3:
time: 138 us; the launch traced here: 137 us
  Pallas kernels  132 us (96%)
  local copies, waits for them, and re-layouts  3.75 us (3%)
    pallas_call x1, Pallas kernels, per_device(): pl.pallas_call(functools.partial(kernel, nx, ny, nz), out_shape=(jax.Shap...  132 us
    unnamed x4, local copies, waits for them, and re-layouts  3.75 us

profile of v3, /device:TPU:1, one launch (start us, length us, event | category | flops | bytes accessed | tf_op | source)
XLA Modules:
  0.0 137.5 jit_solution(8815518319023663593)
XLA Ops:
  1.3 132.5 %shard_map.77 = (f32[4096,64]{1,0:T(8,128)}, bf16[64,512]{1,0:T(8,128)(2,1)}) custom-call(s32[1,1,1]{2,1,0:T(1,128)S(6)} %copy.10.live_ref, f32[4096,64]{1,0:T(8,128)} %bitcast.9, bf16[4096,512]{1,0:T(8,128)(2,1)} %bitcast.7, bf16[512,256]{1,0:T(8,128)(2,1)} %constant.6.clone.pack_hbm, bf16[1536,512]{1,0:T(8,128)(2,1)} %constant.7.clone.full_hbm, ...), custom_call_target="tpu_custom_call" | custom-call | tf_op jit(solution)/shard_map/pallas_call | solution.py:493
  133.7 0.0 copy-start
  133.7 3.1 %copy.11 = f32[64,8,16,32]{0,3,2,1:T(8,128)} copy(f32[64,8,16,32]{0,3,2,1:T(8,128)} %bitcast.8) | data formatting | bytes 2097152
  136.9 0.0 copy-done
  136.9 0.6 copy.12
Async XLA Ops:
  133.7 3.1 %copy-start = (bf16[64,512]{1,0:T(8,128)(2,1)S(1)}, bf16[64,512]{1,0:T(8,128)(2,1)}, u32[]{:S(2)}) copy-start(bf16[64,512]{1,0:T(8,128)(2,1)} %get-tuple-element.9) | copy-start | bytes 196612
